TPU v7x, 128 devices: a whole 4x4x4 slice. The times are simulated.
128 devices in a mesh: dom: 8 (over z, core), bulk: 16 (over x, y).
Axes of the slice: x: 4, y: 4, z: 4, core: 2. Of those that a mesh axis runs over, the one named last changes fastest.
Arguments:
- node_patch: int32 [2097152], P(('dom', 'bulk')), may hold values from 0 to 39999, as said below
- node_span: int32 [2097152], P(('dom', 'bulk')), may hold values from 0 to 15
- start_grid: int32 [2, 2097152], P(None, ('dom', 'bulk')), may hold values from 0 to 15
- target: float32 [3, 2097152], P(None, ('dom', 'bulk')), may hold values from -0.1 to 1.1
- net: float32 [40000, 1024], P('bulk'), as said below
Outputs:
- placed: float32 [9, 2097152], P(None, ('dom', 'bulk'))
Inputs may be any that keep to these rules, and one draw needn't show every extreme that they name: In each partition's block of 16384 nodes (block k of the array, dom slowest), no owner node_patch // 2500 is named by more than 2560 nodes, and one owner is named by exactly 2560; that owner is the same for all blocks of one index of dom. `net`: component 3 (the weight) of every control point is positive.
All inputs are finite; a program needn't handle non-finite values.
Results may differ from a plain program's by a relative error of at most 0.0003.
Values sent between devices are 32-bit elements; how exact they have to be, the bound alone decides.
A program may use at most 128 MiB of HBM per device.

v0:
```python
import jax
import jax.numpy as jnp
from jax import lax
from jax.sharding import PartitionSpec as P

SPANS = 16
LEVELS = 16
ITERS = 4


damping = 0.1
highest = lax.Precision.HIGHEST


def bernstein(param):
    other = 1.0 - param
    value = jnp.stack(
        [
            other * other * other,
            3.0 * param * other * other,
            3.0 * param * param * other,
            param * param * param,
        ]
    )
    slope = jnp.stack(
        [
            -3.0 * other * other,
            3.0 * other * other - 6.0 * param * other,
            6.0 * param * other - 3.0 * param * param,
            3.0 * param * param,
        ]
    )
    return (value, slope)


def surface(control, upar, vpar):
    base_u, slope_u = bernstein(upar)
    basis_along_vdir, slope_vdir = bernstein(vpar)
    mixed_partial = jnp.sum(base_u[None, :, None, :] * control, axis=1)
    mixed_partial_udir = jnp.sum(slope_u[None, :, None, :] * control, axis=1)
    homogeneous_point = jnp.sum(basis_along_vdir[None] * mixed_partial, axis=1)
    homogeneous_udiff = jnp.sum(basis_along_vdir[None] * mixed_partial_udir, axis=1)
    homogeneous_vdiff = jnp.sum(slope_vdir[None] * mixed_partial, axis=1)
    rational_weight = homogeneous_point[3]
    surface_point = homogeneous_point[:3] / rational_weight
    tangent_udir = (homogeneous_udiff[:3] - surface_point * homogeneous_udiff[3]) / rational_weight
    tangent_vdir = (homogeneous_vdiff[:3] - surface_point * homogeneous_vdiff[3]) / rational_weight
    return (surface_point, tangent_udir, tangent_vdir)


def project(coeffs, goal, start):
    control = coeffs.reshape(4, 4, 4, -1)
    upar = start[0]
    vpar = start[1]
    for step in range(ITERS):
        surface_point, tangent_udir, tangent_vdir = surface(control, upar, vpar)
        miss = surface_point - goal
        grad_u = jnp.sum(tangent_udir * miss, axis=0)
        grad_v = jnp.sum(tangent_vdir * miss, axis=0)
        h_uu = jnp.sum(tangent_udir * tangent_udir, axis=0) + damping
        h_vv = jnp.sum(tangent_vdir * tangent_vdir, axis=0) + damping
        h_uv = jnp.sum(tangent_udir * tangent_vdir, axis=0)
        determ = h_uu * h_vv - h_uv * h_uv
        upar = jnp.clip(upar - (h_vv * grad_u - h_uv * grad_v) / determ, 0.0, 1.0)
        vpar = jnp.clip(vpar - (h_uu * grad_v - h_uv * grad_u) / determ, 0.0, 1.0)
    surface_point, tangent_udir, tangent_vdir = surface(control, upar, vpar)
    return jnp.concatenate([surface_point, tangent_udir, tangent_vdir], axis=0)


def rank_within(byowner):
    nodes, owners = byowner.shape
    block = min(512, nodes)
    count = nodes // block
    grouped = byowner.reshape(count, block, owners)
    lower = (jnp.arange(block)[:, None] > jnp.arange(block)[None, :]).astype(jnp.float32)
    inner = jnp.einsum("ij,bjo->bio", lower, grouped, precision=highest)
    totals = jnp.sum(grouped, axis=1)
    offsets = jnp.cumsum(totals, axis=0) - totals
    before = (inner + offsets[:, None, :]).reshape(nodes, owners)
    return jnp.sum(before * byowner, axis=1)


def to_slots(values, byowner, byslot):
    masked = values[:, None, :] * byowner.T[None, :, :]
    rows, owners, nodes = masked.shape
    placed = jnp.dot(masked.reshape(rows * owners, nodes), byslot, precision=highest)
    return placed.reshape(rows, owners, -1)


def from_slots(slotted, byowner, byslot):
    rows, owners, capacity = slotted.shape
    spread = jnp.dot(slotted.reshape(rows * owners, capacity), byslot.T, precision=highest)
    spread = spread.reshape(rows, owners, -1)
    return jnp.sum(spread * byowner.T[None, :, :], axis=1)


def body(node_patch, node_span, start_grid, target, net):
    owners = lax.axis_size("bulk")
    patch_dev = net.shape[0]
    nodes = node_patch.shape[0]
    capacity = nodes * 5 // 32
    owner = node_patch // patch_dev
    local_row = (node_patch - owner * patch_dev) * SPANS + node_span
    byowner = (owner[:, None] == jnp.arange(owners, dtype=jnp.int32)[None, :]).astype(jnp.float32)
    within = rank_within(byowner).astype(jnp.int32)
    byslot = (within[:, None] == jnp.arange(capacity, dtype=jnp.int32)[None, :]).astype(jnp.float32)
    net_rows = net.reshape(-1, 64)
    start = (start_grid.astype(jnp.float32) + 0.5) / LEVELS
    payload = jnp.concatenate([target, start, local_row.astype(jnp.float32)[None]], axis=0)
    outgoing = to_slots(payload, byowner, byslot)
    received = lax.all_to_all(outgoing, "bulk", split_axis=1, concat_axis=1, tiled=True)
    count = received.shape[2]
    rows = received[5].astype(jnp.int32).reshape(-1)
    coeffs = net_rows[rows].T
    result = project(coeffs, received[0:3].reshape(3, -1), received[3:5].reshape(2, -1))
    answered = lax.all_to_all(
        result.reshape(9, owners, count), "bulk", split_axis=1, concat_axis=1, tiled=True
    )
    return from_slots(answered, byowner, byslot)


def solution(mesh):
    return jax.shard_map(
        body,
        mesh=mesh,
        in_specs=(
            P(("dom", "bulk")),
            P(("dom", "bulk")),
            P(None, ("dom", "bulk")),
            P(None, ("dom", "bulk")),
            P("bulk", None),
        ),
        out_specs=P(None, ("dom", "bulk")),
        check_vma=False,
    )
```

profile of v0, /device:TPU:0, one launch (start us, length us, event | category | flops | bytes accessed | tf_op | source)
XLA Modules:
  0.0 527.7 jit_solution(6369307458620404501)
XLA Ops:
  2.8 70.5 %fusion.3 = f32[6,16,2560]{2,1,0:T(8,128)S(1)} fusion(s32[16384]{0:T(1024)S(1)} %bitcast.100, f32[6,16,16384]{2,1,0:T(8,128)S(1)} %fusion.72), kind=kOutput, calls=%fused_computation.4 | convolution fusion | flops 48360325120 | bytes 7340032 | tf_op jit(solution)/shard_map/dot_general | solution.py:86
  73.3 1.7 copy.24
  75.0 7.1 %all-to-all-start = ((f32[6,16,2560]{2,0,1:T(8,128)}), f32[6,16,2560]{2,0,1:T(8,128)S(1)}, u32[]{:S(2)}, u32[]{:S(2)}) async-start(f32[6,16,2560]{2,0,1:T(8,128)} %copy.24), calls=%async_computation | async-start | bytes 2621440 | tf_op jit(solution)/shard_map/all_to_all | solution.py:111
  82.1 16.0 %reshape.4551 = f32[40000,64]{1,0:T(8,128)} reshape(f32[2500,1024]{1,0:T(8,128)} %param.9) | data formatting | bytes 20480000 | tf_op jit(solution)/shard_map/reshape | solution.py:107
  98.1 4.8 all-to-all-done
  103.5 141.8 %gather_fusion = f32[40960,64]{1,0:T(8,128)} fusion(f32[40000,64]{1,0:T(8,128)} %reshape.4551, s32[40960]{0:T(1024)S(1)} %broadcast_clamp_fusion), kind=kCustom, calls=%fused_computation | custom fusion | bytes 21135360 | tf_op jit(solution)/shard_map/gather | solution.py:114
  245.3 15.7 %copy.25 = f32[64,40960]{1,0:T(8,128)} copy(f32[64,40960]{0,1:T(8,128)} %bitcast.59) | data formatting | bytes 20971520 | tf_op jit(solution)/shard_map/transpose | solution.py:114
  261.0 11.2 %reshape.4552 = f32[4,4,4,40960]{3,2,1,0:T(4,128)} reshape(f32[64,40960]{1,0:T(8,128)} %copy.25) | data formatting | bytes 20971520 | tf_op jit(solution)/shard_map/reshape | solution.py:52
  275.1 9.9 %multiply_reduce_fusion.8 = (f32[4,4,40960]{2,1,0:T(4,128)S(1)}, f32[4,4,40960]{2,1,0:T(4,128)S(1)}) fusion(f32[4,4,4,40960]{3,2,1,0:T(4,128)} %reshape.4552, f32[4,40960]{1,0:T(4,128)S(1)} %get-tuple-element.163, f32[4,40960]{1,0:T(4,128)S(1)} %get-tuple-element.162), kind=kLoop, calls=%fused_computation.16 | loop fusion | flops 9175040 | bytes 17039360 | tf_op jit(solution)/shard_map/reduce_sum | solution.py:39
  286.2 5.4 %multiply_reduce_fusion.22 = (f32[4,40960]{1,0:T(4,128)S(1)}, f32[4,40960]{1,0:T(4,128)S(1)}, f32[4,40960]{1,0:T(4,128)S(1)}) fusion(f32[4,4,40960]{2,1,0:T(4,128)S(1)} %get-tuple-element.13, f32[4,40960]{1,0:T(4,128)S(1)} %get-tuple-element.165, f32[4,40960]{1,0:T(4,128)S(1)} %get-tuple-element.164, f32[4,4,40960]{2,1,0:T(4,128)S(1)} %get-tuple-element.14), kind=kLoop, calls=%fused_computation.34 | loop fusion | flops 3440640 | bytes 8519680 | tf_op jit(solution)/shard_map/reduce_sum | solution.py:43
  292.8 2.3 multiply_reduce_fusion.41
  298.7 8.1 %multiply_reduce_fusion.6 = (f32[4,4,40960]{2,1,0:T(4,128)S(1)}, f32[4,4,40960]{2,1,0:T(4,128)}) fusion(f32[4,4,4,40960]{3,2,1,0:T(4,128)S(1)} %bitcast.58, f32[4,40960]{1,0:T(4,128)S(1)} %pad_maximum_fusion.7, f32[4,40960]{1,0:T(4,128)S(1)} %pad_maximum_fusion.6), kind=kLoop, calls=%fused_computation.14 | loop fusion | flops 9175040 | bytes 17039360 | tf_op jit(solution)/shard_map/reduce_sum | solution.py:39
  309.7 7.6 %multiply_reduce_fusion.19 = (f32[4,40960]{1,0:T(4,128)S(1)}, f32[4,40960]{1,0:T(4,128)S(1)}, f32[4,40960]{1,0:T(4,128)S(1)}) fusion(f32[4,4,40960]{2,1,0:T(4,128)S(1)} %get-tuple-element.11, f32[4,40960]{1,0:T(4,128)} %pad_maximum_fusion.8, f32[4,40960]{1,0:T(4,128)} %pad_maximum_fusion.5, f32[4,4,40960]{2,1,0:T(4,128)} %get-tuple-element.12), kind=kLoop, calls=%fused_computation.31 | loop fusion | flops 3440640 | bytes 8519680 | tf_op jit(solution)/shard_map/reduce_sum | solution.py:43
  318.3 2.3 multiply_reduce_fusion.36
  324.4 8.1 %multiply_reduce_fusion.4 = (f32[4,4,40960]{2,1,0:T(4,128)S(1)}, f32[4,4,40960]{2,1,0:T(4,128)}) fusion(f32[4,4,4,40960]{3,2,1,0:T(4,128)S(1)} %bitcast.58, f32[4,40960]{1,0:T(4,128)S(1)} %pad_maximum_fusion.11, f32[4,40960]{1,0:T(4,128)S(1)} %pad_maximum_fusion.10), kind=kLoop, calls=%fused_computation.12 | loop fusion | flops 9175040 | bytes 17039360 | tf_op jit(solution)/shard_map/reduce_sum | solution.py:39
  335.4 7.6 %multiply_reduce_fusion.16 = (f32[4,40960]{1,0:T(4,128)S(1)}, f32[4,40960]{1,0:T(4,128)S(1)}, f32[4,40960]{1,0:T(4,128)S(1)}) fusion(f32[4,4,40960]{2,1,0:T(4,128)S(1)} %get-tuple-element.9, f32[4,40960]{1,0:T(4,128)} %pad_maximum_fusion.12, f32[4,40960]{1,0:T(4,128)} %pad_maximum_fusion.9, f32[4,4,40960]{2,1,0:T(4,128)} %get-tuple-element.10), kind=kLoop, calls=%fused_computation.28 | loop fusion | flops 3440640 | bytes 8519680 | tf_op jit(solution)/shard_map/reduce_sum | solution.py:43
  344.0 2.3 multiply_reduce_fusion.31
  349.8 8.1 %multiply_reduce_fusion.2 = (f32[4,4,40960]{2,1,0:T(4,128)S(1)}, f32[4,4,40960]{2,1,0:T(4,128)}) fusion(f32[4,4,4,40960]{3,2,1,0:T(4,128)S(1)} %bitcast.58, f32[4,40960]{1,0:T(4,128)S(1)} %pad_maximum_fusion.15, f32[4,40960]{1,0:T(4,128)S(1)} %pad_maximum_fusion.14), kind=kLoop, calls=%fused_computation.10 | loop fusion | flops 9175040 | bytes 17039360 | tf_op jit(solution)/shard_map/reduce_sum | solution.py:39
  360.9 7.6 %multiply_reduce_fusion.13 = (f32[4,40960]{1,0:T(4,128)S(1)}, f32[4,40960]{1,0:T(4,128)S(1)}, f32[4,40960]{1,0:T(4,128)S(1)}) fusion(f32[4,4,40960]{2,1,0:T(4,128)S(1)} %get-tuple-element.7, f32[4,40960]{1,0:T(4,128)} %pad_maximum_fusion.16, f32[4,40960]{1,0:T(4,128)} %pad_maximum_fusion.13, f32[4,4,40960]{2,1,0:T(4,128)} %get-tuple-element.8), kind=kLoop, calls=%fused_computation.25 | loop fusion | flops 3440640 | bytes 8519680 | tf_op jit(solution)/shard_map/reduce_sum | solution.py:43
  369.4 2.3 multiply_reduce_fusion.26
  375.5 6.6 %multiply_reduce_fusion = (f32[4,4,40960]{2,1,0:T(4,128)S(1)}, f32[4,4,40960]{2,1,0:T(4,128)S(1)}) fusion(f32[4,4,4,40960]{3,2,1,0:T(4,128)S(1)} %bitcast.58, f32[4,40960]{1,0:T(4,128)S(1)} %pad_maximum_fusion.19, f32[4,40960]{1,0:T(4,128)S(1)} %pad_maximum_fusion.18), kind=kLoop, calls=%fused_computation.8 | loop fusion | flops 9175040 | bytes 17039360 | tf_op jit(solution)/shard_map/reduce_sum | solution.py:40
  383.4 5.4 %multiply_reduce_fusion.12 = (f32[4,40960]{1,0:T(4,128)S(1)}, f32[4,40960]{1,0:T(4,128)S(1)}, f32[4,40960]{1,0:T(4,128)S(1)}) fusion(f32[4,4,40960]{2,1,0:T(4,128)S(1)} %get-tuple-element.6, f32[4,40960]{1,0:T(4,128)S(1)} %pad_maximum_fusion.17, f32[4,40960]{1,0:T(4,128)S(1)} %pad_maximum_fusion.20, f32[4,4,40960]{2,1,0:T(4,128)S(1)} %get-tuple-element.5), kind=kLoop, calls=%fused_computation.24 | loop fusion | flops 3440640 | bytes 8519680 | tf_op jit(solution)/shard_map/reduce_sum | solution.py:41
  393.2 35.7 %all_to_all.10 = f32[9,16,2560]{2,0,1:T(8,128)S(1)} all-to-all(f32[9,16,2560]{2,0,1:T(8,128)S(1)} %copy.26), channel_id=1, replica_groups=mesh['dom'=8,'bulk'=16] {'bulk'}, dimensions={1} | all-to-all | bytes 2949120 | tf_op jit(solution)/shard_map/all_to_all | solution.py:116
  429.0 98.5 %fusion.13 = f32[9,16384]{1,0:T(8,128)} fusion(f32[16,16384]{1,0:T(8,128)S(1)} %copy-done.1, s32[16384]{0:T(1024)S(1)} %bitcast.101, f32[9,16,2560]{2,0,1:T(8,128)S(1)} %all_to_all.10), kind=kOutput, calls=%fused_computation.37 | convolution fusion | flops 72524087296 | bytes 3178496 | tf_op jit(solution)/shard_map/dot_general | solution.py:92
  (103 shorter events, 40.2 us)
Async XLA Ops:
  0.0 2.0 copy-start.5
  0.0 2.1 copy-start.4
  1.1 1.8 copy-start
  2.0 0.8 copy-start.6
  75.0 27.9 %all-to-all-start = ((f32[6,16,2560]{2,0,1:T(8,128)}), f32[6,16,2560]{2,0,1:T(8,128)S(1)}, u32[]{:S(2)}, u32[]{:S(2)}) async-start(f32[6,16,2560]{2,0,1:T(8,128)} %copy.24), calls=%async_computation | async-start | bytes 2621440 | tf_op jit(solution)/shard_map/all_to_all | solution.py:111
  286.2 12.4 %slice-start = ((s8[10485760]{0:T(1024)(128)(4,1)}), s8[4194304]{0:T(1024)(128)(4,1)S(1)}, s32[]{:S(2)}) async-start(s8[10485760]{0:T(1024)(128)(4,1)} %bitcast.57), calls=%async_computation.2 | async-start | bytes 8388608
  291.6 7.0 %slice-start.1 = ((s8[10485760]{0:T(1024)(128)(4,1)}), s8[4194304]{0:T(1024)(128)(4,1)S(1)}, s32[]{:S(2)}) async-start(s8[10485760]{0:T(1024)(128)(4,1)} %bitcast.57), calls=%async_computation.3 | async-start | bytes 8388608
  292.8 5.9 %slice-start.2 = ((s8[10485760]{0:T(1024)(128)(4,1)}), s8[2097152]{0:T(1024)(128)(4,1)S(1)}, s32[]{:S(2)}) async-start(s8[10485760]{0:T(1024)(128)(4,1)} %bitcast.57), calls=%async_computation.4 | async-start | bytes 4194304
  322.4 1.3 copy-start.2
  344.0 3.6 copy-start.3
  393.2 35.8 %copy-start.1 = (f32[16,16384]{1,0:T(8,128)S(1)}, f32[16,16384]{1,0:T(8,128)}, u32[]{:S(2)}) copy-start(f32[16,16384]{1,0:T(8,128)} %copy-done) | copy-start | bytes 3145732
  393.2 35.8 %copy-start.7 = (s32[4,4,8,128]{3,1,2,0:T(4,128)S(1)}, s32[4,4,8,128]{3,1,2,0:T(4,128)}, u32[]{:S(2)}) copy-start(s32[4,4,8,128]{3,1,2,0:T(4,128)} %copy-done.6) | copy-start | bytes 196612
where the time goes:
time: 537 us; the launch traced here: 528 us
  local copies, waits for them, and re-layouts  192 us (36%)
  matrix products  170 us (32%)
  other arithmetic  118 us (22%)
  blocking collectives  35.7 us (7%)
  starting transfers between devices  7.12 us (1%)
    gather x1, local copies, waits for them, and re-layouts, body(): coeffs = net_rows[rows].T  142 us
    dot_general x1, matrix products, from_slots(): jnp.dot(slotted.reshape(rows * owners, capacity), byslot.T, precision=hig...  98.5 us
    dot_general x1, matrix products, to_slots(): jnp.dot(masked.reshape(rows * owners, nodes), byslot, precision=highest)  70.5 us
    all_to_all x1, blocking collectives, body(): lax.all_to_all(result.reshape(9, owners, count), 'bulk', split_axis=1, co...  35.7 us
    reduce_sum x4, other arithmetic, surface(): mixed_partial = jnp.sum(base_u[None, :, None, :] * control, axis=1)  34.2 us
    reduce_sum x4, other arithmetic, surface(): homogeneous_vdiff = jnp.sum(slope_vdir[None] * mixed_partial, axis=1)  28 us
    reshape x1, local copies, waits for them, and re-layouts, body(): net_rows = net.reshape(-1, 64)  16 us
    transpose x1, local copies, waits for them, and re-layouts, body(): coeffs = net_rows[rows].T  15.7 us
  transfers between devices with their start and end apart: 1, of which 1 were waited for; matrix products, arithmetic and copies ran while one was open for 3% of the time, Pallas kernels for 0%

commit v1 on v0

v1 whole, which is shorter than its diff:
```python
import functools

import jax
import jax.numpy as jnp
import numpy as np
from jax import lax
from jax.experimental import pallas as pl
from jax.experimental.pallas import tpu as pltpu
from jax.sharding import PartitionSpec as P

F32 = jnp.float32
BF16 = jnp.bfloat16
I32 = jnp.int32
MESH = pl.DeviceIdType.MESH

SPANS = 16
LEVELS = 16
ITERS = 4
DAMPING = 0.1
OWNERS = 16
PATCH_DEV = 2500
PITCH = 2504
TILES = 20
GROUPS = OWNERS * TILES
MARGIN = 3
BATCH = 8


def iota(shape, dim):
    return lax.broadcasted_iota(I32, shape, dim)


def split3(x):
    high = x.astype(BF16)
    rest = x - high.astype(F32)
    mid = rest.astype(BF16)
    low = (rest - mid.astype(F32)).astype(BF16)
    return jnp.concatenate([high, mid, low], 0)


def block_permutation(place_ref, j):
    place = jnp.concatenate([place_ref[pl.ds(j, 1), :], place_ref[pl.ds(j + 64, 1), :]], 1)
    return jnp.where(iota((256, 256), 0).astype(F32) == place, 1.0, 0.0).astype(BF16)


def dispatch_kernel(patch_ref, span_ref, start_ref, target_ref, out_ref, place_ref, table_ref,
                    code_ref, values, stage, table_v, table_s, sem):
    patch = patch_ref[...]
    span = span_ref[...]
    owner = ((patch.astype(F32) + 0.5) * (1.0 / PATCH_DEV)).astype(I32)
    local = patch - owner * PATCH_DEV
    code_ref[...] = (((span >> 1) * PITCH + local) * 2 + (span & 1)).astype(F32)
    upper = (iota((128, 128), 0) < iota((128, 128), 1)).astype(F32)
    upper = jnp.concatenate([upper, jnp.ones((128, 128), F32)], 1).astype(BF16)
    lower = (iota((64, 64), 0) > iota((64, 64), 1)).astype(F32).astype(BF16)
    lane = iota((64, 128), 1)
    begin = jnp.zeros((64, 128), F32)
    place = jnp.zeros((128, 128), F32)
    table = jnp.zeros((64, 128), I32)
    for o in range(OWNERS):
        mine = (owner == o).astype(F32)
        both = jnp.dot(mine.astype(BF16), upper, preferred_element_type=F32)
        earlier, total = both[:, :128], both[:, 128:]
        count = total[:64] + total[64:]
        base = jnp.dot(lower, count.astype(BF16), preferred_element_type=F32).astype(I32)
        place += mine * jnp.concatenate([earlier[:64] + begin, earlier[64:] + total[:64] + begin], 0)
        first = begin.astype(I32)
        offset = base & 127
        columns = ((offset - first) & 255, offset, base >> 7, offset + count.astype(I32),
                   first, (first - offset) & 255)
        for k, column in enumerate(columns):
            table = jnp.where(lane == k * OWNERS + o, column, table)
        begin = begin + count
    place_ref[...] = place
    table_v[...] = table
    table_ref[...] = table
    copy = pltpu.make_async_copy(table_v, table_s, sem)
    copy.start()
    values[0:3, :] = target_ref[...]
    values[3:5, :] = (start_ref[...].astype(F32) + 0.5) * (1.0 / LEVELS)
    values[5:8, :] = jnp.zeros((3, values.shape[1]), F32)
    stage[...] = jnp.zeros_like(stage)
    copy.wait()
    row = iota((8, 128), 0)
    lane = iota((8, 128), 1)

    def body(j, current):
        halves = []
        for h in range(2):
            r = j + 64 * h
            x = values[:, pl.ds(pl.multiple_of(r * 128, 128), 128)]
            halves.append(jnp.where(row == 5, code_ref[pl.ds(r, 8, stride=0), :], x))
        x = split3(jnp.concatenate(halves, 1))
        y = lax.dot_general(x, block_permutation(place_ref, j), (((1,), (1,)), ((), ())),
                            preferred_element_type=F32)
        y = y[0:8] + y[8:16] + y[16:24]
        following = []
        for o in range(OWNERS):
            rolled = pltpu.roll(y, table_s[j, o], axis=1)
            left, right = rolled[:, :128], rolled[:, 128:]
            offset, tile, end = table_s[j, 16 + o], table_s[j, 32 + o], table_s[j, 48 + o]
            merged = jnp.where(lane >= offset, left, current[o])
            at = pl.multiple_of((o * (TILES + MARGIN) + tile) * 8, 8)
            stage[pl.ds(at, 8), :] = merged
            stage[pl.ds(at + 8, 8), :] = right
            stage[pl.ds(at + 16, 8), :] = left
            following.append(jnp.where(end < 128, merged, jnp.where(end < 256, right, left)))
        return tuple(following)

    lax.fori_loop(0, 64, body, tuple(jnp.zeros((8, 128), F32) for _ in range(OWNERS)))
    for o in range(OWNERS):
        out_ref[o] = stage[pl.ds(o * (TILES + MARGIN) * 8, TILES * 8), :]


def dispatch(patch, span, start, target):
    vmem = pl.BlockSpec(memory_space=pltpu.VMEM)
    return pl.pallas_call(
        dispatch_kernel,
        out_shape=[
            jax.ShapeDtypeStruct((OWNERS, TILES * 8, 128), F32),
            jax.ShapeDtypeStruct((128, 128), F32),
            jax.ShapeDtypeStruct((64, 128), I32),
        ],
        in_specs=[vmem] * 4,
        out_specs=[vmem] * 3,
        scratch_shapes=[
            pltpu.VMEM((128, 128), F32),
            pltpu.VMEM((8, 16384), F32),
            pltpu.VMEM((OWNERS * (TILES + MARGIN) * 8, 128), F32),
            pltpu.VMEM((64, 128), I32),
            pltpu.SMEM((64, 128), I32),
            pltpu.SemaphoreType.DMA,
        ],
        compiler_params=pltpu.CompilerParams(vmem_limit_bytes=32 << 20),
        name="dispatch",
    )(patch.reshape(128, 128), span.reshape(128, 128), start, target)


def exchange_kernel(count, *refs):
    sources, targets = refs[:count], refs[count:2 * count]
    send, recv, own = refs[2 * count:]
    me = lax.axis_index("bulk")
    barrier = pltpu.get_barrier_semaphore()
    for k in range(1, OWNERS):
        peer = lax.rem(me + k, OWNERS)
        pl.semaphore_signal(barrier, inc=1, device_id={"bulk": peer}, device_id_type=MESH)
    local = [pltpu.make_async_copy(s.at[me], t.at[me], own.at[i])
             for i, (s, t) in enumerate(zip(sources, targets))]
    for copy in local:
        copy.start()
    pl.semaphore_wait(barrier, OWNERS - 1)

    def copies(k, dst):
        peer = lax.rem(me + k, OWNERS)
        return [
            pltpu.make_async_remote_copy(
                src_ref=s.at[peer], dst_ref=t.at[dst],
                send_sem=send.at[i, k], recv_sem=recv.at[i, k],
                device_id={"bulk": peer}, device_id_type=MESH,
            )
            for i, (s, t) in enumerate(zip(sources, targets))
        ]

    for k in range(1, OWNERS):
        for copy in copies(k, me):
            copy.start()
    for copy in local:
        copy.wait()
    for k in range(1, OWNERS):
        for copy in copies(k, lax.rem(me + OWNERS - k, OWNERS)):
            copy.wait()


def exchange(arrays, collective_id):
    count = len(arrays)
    hbm = pl.BlockSpec(memory_space=pl.ANY)
    return pl.pallas_call(
        functools.partial(exchange_kernel, count),
        out_shape=[jax.ShapeDtypeStruct(a.shape, a.dtype) for a in arrays],
        in_specs=[hbm] * count,
        out_specs=[hbm] * count,
        scratch_shapes=[
            pltpu.SemaphoreType.DMA((count, OWNERS)),
            pltpu.SemaphoreType.DMA((count, OWNERS)),
            pltpu.SemaphoreType.DMA((count,)),
        ],
        compiler_params=pltpu.CompilerParams(collective_id=collective_id, has_side_effects=True),
        name="exchange%d" % collective_id,
    )(*arrays)


TO_POWERS = np.array([[1, 0, 0, 0], [-3, 3, 0, 0], [3, -6, 3, 0], [-1, 3, -3, 1]], np.float32)


def power_matrix():
    one = np.kron(np.eye(4, dtype=np.float32), np.kron(TO_POWERS, TO_POWERS))
    pair = np.kron(np.eye(2, dtype=np.float32), one)
    return np.concatenate([pair, pair], 1)


def value_slope(a, t):
    b2 = a[3] * t + a[2]
    b1 = b2 * t + a[1]
    return b1 * t + a[0], (a[3] * t + b2) * t + b1


def value_only(a, t):
    return ((a[3] * t + a[2]) * t + a[1]) * t + a[0]


def surface(load, u, v):
    point, along_u, along_v = [], [], []
    for c in range(4):
        values, slopes = [], []
        for j in range(4):
            value, slope = value_slope([load(c * 16 + i * 4 + j) for i in range(4)], u)
            values.append(value)
            slopes.append(slope)
        h, hv = value_slope(values, v)
        point.append(h)
        along_u.append(value_only(slopes, v))
        along_v.append(hv)
    inverse = 1.0 / point[3]
    p = [point[c] * inverse for c in range(3)]
    su = [(along_u[c] - p[c] * along_u[3]) * inverse for c in range(3)]
    sv = [(along_v[c] - p[c] * along_v[3]) * inverse for c in range(3)]
    return p, su, sv


def dot3(a, b):
    return a[0] * b[0] + a[1] * b[1] + a[2] * b[2]


def project(load, goal, u, v):
    for _ in range(ITERS):
        p, su, sv = surface(load, u, v)
        miss = [p[c] - goal[c] for c in range(3)]
        gu, gv = dot3(su, miss), dot3(sv, miss)
        a, d, b = dot3(su, su) + DAMPING, dot3(sv, sv) + DAMPING, dot3(su, sv)
        inverse = 1.0 / (a * d - b * b)
        u, v = (jnp.clip(u - (d * gu - b * gv) * inverse, 0.0, 1.0),
                jnp.clip(v - (a * gv - b * gu) * inverse, 0.0, 1.0))
    return surface(load, u, v)


def project_kernel(recv_ref, net_hbm, powers_ref, main_ref, last_ref,
                   net, index_v, odd, index_s, rows, control, last, sem):
    loads = [
        pltpu.make_async_copy(net_hbm.at[:, pl.ds(k * 128, 128)],
                              net.at[pl.ds(k * PITCH, PATCH_DEV), :], sem.at[k])
        for k in range(8)
    ]
    for copy in loads:
        copy.start()

    def prepare(b, carry):
        code = recv_ref[pl.ds(b * 64 + 5, 8, stride=8), :].astype(I32)
        index_v[pl.ds(b * 8, 8), :] = code >> 1
        odd[pl.ds(b * 8, 8), :] = code & 1
        return carry

    lax.fori_loop(0, GROUPS // BATCH, prepare, 0)
    copy = pltpu.make_async_copy(index_v, index_s, sem.at[8])
    copy.start()
    for each in loads:
        each.wait()
    copy.wait()

    def body(b, carry):
        for g in range(BATCH):
            for t in range(16):
                parts = [net[pl.ds(index_s[b * 8 + g, t * 8 + s], 1), :] for s in range(8)]
                rows[pl.ds(g * 128 + t * 8, 8), :] = jnp.concatenate(parts, 0)
        for h in range(4):
            x = rows[pl.ds(h * 256, 256), :]
            high = x.astype(BF16)
            low = (x - high.astype(F32)).astype(BF16)
            flat = lax.dot_general(powers_ref[...], jnp.concatenate([high, low], 1),
                                   (((1,), (1,)), ((), ())), preferred_element_type=F32)
            for q in range(2):
                which = odd[pl.ds(b * 8 + h * 2 + q, 1), :]
                part = flat[:, q * 128:(q + 1) * 128]
                control[pl.ds((h * 2 + q) * 64, 64), :] = jnp.where(which == 1, part[64:], part[:64])

        def load(k):
            return control[pl.ds(k, 8, stride=64), :]

        def value(k):
            return recv_ref[pl.ds(b * 64 + k, 8, stride=8), :]

        p, su, sv = project(load, [value(0), value(1), value(2)], value(3), value(4))
        for k, x in enumerate((p + su + sv)[:8]):
            main_ref[pl.ds(b * 64 + k, 8, stride=8), :] = x
        last[pl.ds(b * 8, 8), :] = sv[2]
        return carry

    lax.fori_loop(0, GROUPS // BATCH, body, 0)
    for o in range(OWNERS):
        last_ref[o, 0:TILES, :] = last[pl.ds(o * TILES, TILES), :]
        last_ref[o, TILES:24, :] = jnp.zeros((24 - TILES, 128), F32)


def place_nodes(received, net):
    vmem = pl.BlockSpec(memory_space=pltpu.VMEM)
    return pl.pallas_call(
        project_kernel,
        out_shape=[
            jax.ShapeDtypeStruct((GROUPS * 8, 128), F32),
            jax.ShapeDtypeStruct((OWNERS, 24, 128), F32),
        ],
        in_specs=[vmem, pl.BlockSpec(memory_space=pl.ANY), vmem],
        out_specs=[vmem] * 2,
        scratch_shapes=[
            pltpu.VMEM((8 * PITCH, 128), F32),
            pltpu.VMEM((GROUPS, 128), I32),
            pltpu.VMEM((GROUPS, 128), I32),
            pltpu.SMEM((GROUPS, 128), I32),
            pltpu.VMEM((BATCH * 128, 128), F32),
            pltpu.VMEM((BATCH * 64, 128), F32),
            pltpu.VMEM((GROUPS, 128), F32),
            pltpu.SemaphoreType.DMA((9,)),
        ],
        compiler_params=pltpu.CompilerParams(vmem_limit_bytes=48 << 20),
        name="project",
    )(received.reshape(GROUPS * 8, 128), net, jnp.asarray(power_matrix(), BF16))


def collect_kernel(main_hbm, last_hbm, place_ref, table_hbm, out_ref, main, last, table_s, sem):
    copies = [
        pltpu.make_async_copy(main_hbm, main.at[pl.ds(0, GROUPS * 8), :], sem.at[0]),
        pltpu.make_async_copy(last_hbm, last.at[pl.ds(0, OWNERS * 24), :], sem.at[1]),
        pltpu.make_async_copy(table_hbm, table_s, sem.at[2]),
    ]
    for copy in copies:
        copy.start()
    main[pl.ds(GROUPS * 8, 24), :] = jnp.zeros((24, 128), F32)
    for copy in copies:
        copy.wait()
    lane = iota((8, 128), 1)

    def body(j, carry):
        acc = [jnp.zeros((8, 128), F32) for _ in range(4)]
        for o in range(OWNERS):
            offset, tile = table_s[j, 16 + o], table_s[j, 32 + o]
            first, shift = table_s[j, 64 + o], table_s[j, 80 + o]
            keep, low, high = lane >= offset, lane >= first, lane >= first - 128
            at = pl.multiple_of((o * TILES + tile) * 8, 8)
            row = o * 24 + tile
            windows = (
                [main[pl.ds(at + 8 * i, 8), :] for i in range(3)],
                [last[pl.ds(row + i, 8, stride=0), :] for i in range(3)],
            )
            for i, (w0, w1, w2) in enumerate(windows):
                x = jnp.concatenate([jnp.where(keep, w0, w2), w1], 1)
                x = pltpu.roll(x, shift, axis=1)
                acc[2 * i] = jnp.where(low, x[:, :128], acc[2 * i])
                acc[2 * i + 1] = jnp.where(high, x[:, 128:], acc[2 * i + 1])
        x = jnp.concatenate([jnp.concatenate(acc[:2], 1), jnp.concatenate(acc[2:], 1)], 0)
        y = jnp.dot(split3(x), block_permutation(place_ref, j), preferred_element_type=F32)
        y = y[0:16] + y[16:32] + y[32:48]
        for h in range(2):
            at = pl.multiple_of((j + 64 * h) * 128, 128)
            out_ref[:, pl.ds(at, 128)] = y[0:9, h * 128:(h + 1) * 128]
        return carry

    lax.fori_loop(0, 64, body, 0)


def collect(main, last, place, table):
    vmem = pl.BlockSpec(memory_space=pltpu.VMEM)
    hbm = pl.BlockSpec(memory_space=pl.ANY)
    return pl.pallas_call(
        collect_kernel,
        out_shape=jax.ShapeDtypeStruct((9, 16384), F32),
        in_specs=[hbm, hbm, vmem, hbm],
        out_specs=vmem,
        scratch_shapes=[
            pltpu.VMEM((GROUPS * 8 + 24, 128), F32),
            pltpu.VMEM((OWNERS * 24, 128), F32),
            pltpu.SMEM((64, 128), I32),
            pltpu.SemaphoreType.DMA((3,)),
        ],
        compiler_params=pltpu.CompilerParams(vmem_limit_bytes=32 << 20),
        name="collect",
    )(main.reshape(GROUPS * 8, 128), last.reshape(OWNERS * 24, 128), place, table)


def body(node_patch, node_span, start_grid, target, net):
    outgoing, place, table = dispatch(node_patch, node_span, start_grid, target)
    (received,) = exchange([outgoing], 1)
    main, last = place_nodes(received, net)
    main, last = exchange([main.reshape(OWNERS, TILES * 8, 128), last], 2)
    return collect(main, last, place, table)


def solution(mesh):
    return jax.shard_map(
        body,
        mesh=mesh,
        in_specs=(
            P(("dom", "bulk")),
            P(("dom", "bulk")),
            P(None, ("dom", "bulk")),
            P(None, ("dom", "bulk")),
            P("bulk", None),
        ),
        out_specs=P(None, ("dom", "bulk")),
        check_vma=False,
    )
```

time: 537 us -> 161 us (0.30)
  the two profiles are of different devices: /device:TPU:0 before, /device:TPU:36 now
where the time goes in v1:
time: 161 us; the launch traced here: 159 us
  Pallas kernels  149 us (93%)
  local copies, waits for them, and re-layouts  9.9 us (6%)
    pallas_call x1, Pallas kernels, place_nodes(): pl.pallas_call(project_kernel, out_shape=[jax.ShapeDtypeStruct((GROUPS *...  57 us
    pallas_call x2, Pallas kernels, exchange(): pl.pallas_call(functools.partial(exchange_kernel, count), out_shape=[jax....  49.9 us
    pallas_call x1, Pallas kernels, dispatch(): pl.pallas_call(dispatch_kernel, out_shape=[jax.ShapeDtypeStruct((OWNERS,...  22.8 us
    pallas_call x1, Pallas kernels, collect(): pl.pallas_call(collect_kernel, out_shape=jax.ShapeDtypeStruct((9, 16384),...  19.2 us
    unnamed x22, local copies, waits for them, and re-layouts  9.9 us

profile of v1, /device:TPU:36, one launch (start us, length us, event | category | flops | bytes accessed | tf_op | source)
XLA Modules:
  0.0 158.9 jit_solution(10825194282593929997)
XLA Ops:
  0.0 0.0 copy-start.4
  0.0 0.9 copy-done.4
  1.0 0.0 copy-start.7
  1.0 0.9 copy-done.7
  1.9 0.0 copy-start.9
  1.9 0.8 copy-done.9
  2.7 0.0 copy-start.10
  2.7 0.8 copy-done.10
  3.5 22.8 %dispatch.1 = (f32[16,160,128]{2,1,0:T(8,128)S(1)}, f32[128,128]{1,0:T(8,128)S(1)}, s32[64,128]{1,0:T(8,128)S(1)}) custom-call(s32[128,128]{1,0:T(8,128)S(1)} %bitcast.10, s32[128,128]{1,0:T(8,128)S(1)} %bitcast.11, s32[2,16384]{1,0:T(2,128)S(1)} %copy-done.7, f32[3,16384]{1,0:T(4,128)S(1)} %copy-done.4), custom_call_target="tpu_custom_call" | custom-call | tf_op jit(solution)/shard_map/dispatch/pallas_call | solution.py:117
  26.3 0.0 copy-start.2
  26.3 1.1 copy-done.2
  27.4 23.2 %exchange1.1 = f32[16,160,128]{2,1,0:T(8,128)} custom-call(f32[16,160,128]{2,1,0:T(8,128)} %copy-done.2), custom_call_target="tpu_custom_call" | custom-call | tf_op jit(solution)/shard_map/exchange1/pallas_call | solution.py:177
  50.6 0.0 copy-done.8
  50.6 0.0 copy-start
  50.6 1.3 copy-done
  51.9 57.0 %project.1 = (f32[2560,128]{1,0:T(8,128)S(1)}, f32[16,24,128]{2,1,0:T(8,128)S(1)}) custom-call(f32[2560,128]{1,0:T(8,128)S(1)} %bitcast.6, f32[2500,1024]{1,0:T(8,128)} %net_hbm.1, bf16[128,256]{1,0:T(8,128)(2,1)S(1)} %copy-done.8), custom_call_target="tpu_custom_call" | custom-call | tf_op jit(solution)/shard_map/project/pallas_call | solution.py:305
  109.0 0.0 copy-start.1
  109.0 1.1 copy-done.1
  110.0 0.7 copy-done.5
  110.7 26.7 %exchange2.1 = (f32[16,160,128]{2,1,0:T(8,128)}, f32[16,24,128]{2,1,0:T(8,128)}) custom-call(f32[16,160,128]{2,1,0:T(8,128)} %bitcast.7, f32[16,24,128]{2,1,0:T(8,128)} %copy-done.5), custom_call_target="tpu_custom_call" | custom-call | tf_op jit(solution)/shard_map/exchange2/pallas_call | solution.py:177
  137.4 0.0 copy-start.3
  137.4 1.3 copy-done.3
  138.7 0.9 copy-done.6
  139.6 19.2 %collect.1 = f32[9,16384]{1,0:T(8,128)} custom-call(f32[2560,128]{1,0:T(8,128)S(1)} %bitcast.8, f32[384,128]{1,0:T(8,128)S(1)} %bitcast.9, f32[128,128]{1,0:T(8,128)S(1)} %get-tuple-element.17.place_ref, s32[64,128]{1,0:T(8,128)S(1)} %get-tuple-element.18.table_hbm), custom_call_target="tpu_custom_call" | custom-call | tf_op jit(solution)/shard_map/collect/pallas_call | solution.py:372
  (3 shorter events, 0.0 us)
Async XLA Ops:
  0.0 0.9 copy-start.4
  1.0 0.9 copy-start.7
  1.9 0.8 copy-start.9
  2.7 0.8 copy-start.10
  26.3 1.1 copy-start.2
  27.4 23.2 %copy-start.8 = (bf16[128,256]{1,0:T(8,128)(2,1)S(1)}, bf16[128,256]{1,0:T(8,128)(2,1)}, u32[]{:S(2)}) copy-start(bf16[128,256]{1,0:T(8,128)(2,1)} %constant.2.clone.powers_ref) | copy-start | bytes 196612
  50.6 1.3 copy-start
  109.0 1.1 copy-start.1
  110.0 0.7 copy-start.5
  137.4 1.3 copy-start.3
  138.7 0.9 copy-start.6

commit v2 on v1

--- a/solution.py
+++ b/solution.py
@@ -1,8 +1,5 @@
-import functools
-
 import jax
 import jax.numpy as jnp
-import numpy as np
 from jax import lax
 from jax.experimental import pallas as pl
 from jax.experimental.pallas import tpu as pltpu
@@ -20,10 +17,14 @@
 OWNERS = 16
 PATCH_DEV = 2500
 PITCH = 2504
+TABLE = 8 * PITCH
 TILES = 20
 GROUPS = OWNERS * TILES
 MARGIN = 3
 BATCH = 8
+SLOT = TILES * 8
+PAIR_BATCHES = 2 * TILES // BATCH
+BATCHES = GROUPS // BATCH
 
 
 def iota(shape, dim):
@@ -49,7 +50,7 @@
     span = span_ref[...]
     owner = ((patch.astype(F32) + 0.5) * (1.0 / PATCH_DEV)).astype(I32)
     local = patch - owner * PATCH_DEV
-    code_ref[...] = (((span >> 1) * PITCH + local) * 2 + (span & 1)).astype(F32)
+    code_ref[...] = ((span & 1) * TABLE + (span >> 1) * PITCH + local).astype(F32)
     upper = (iota((128, 128), 0) < iota((128, 128), 1)).astype(F32)
     upper = jnp.concatenate([upper, jnp.ones((128, 128), F32)], 1).astype(BF16)
     lower = (iota((64, 64), 0) > iota((64, 64), 1)).astype(F32).astype(BF16)
@@ -136,66 +137,11 @@
     )(patch.reshape(128, 128), span.reshape(128, 128), start, target)
 
 
-def exchange_kernel(count, *refs):
-    sources, targets = refs[:count], refs[count:2 * count]
-    send, recv, own = refs[2 * count:]
-    me = lax.axis_index("bulk")
-    barrier = pltpu.get_barrier_semaphore()
-    for k in range(1, OWNERS):
-        peer = lax.rem(me + k, OWNERS)
-        pl.semaphore_signal(barrier, inc=1, device_id={"bulk": peer}, device_id_type=MESH)
-    local = [pltpu.make_async_copy(s.at[me], t.at[me], own.at[i])
-             for i, (s, t) in enumerate(zip(sources, targets))]
-    for copy in local:
-        copy.start()
-    pl.semaphore_wait(barrier, OWNERS - 1)
-
-    def copies(k, dst):
-        peer = lax.rem(me + k, OWNERS)
-        return [
-            pltpu.make_async_remote_copy(
-                src_ref=s.at[peer], dst_ref=t.at[dst],
-                send_sem=send.at[i, k], recv_sem=recv.at[i, k],
-                device_id={"bulk": peer}, device_id_type=MESH,
-            )
-            for i, (s, t) in enumerate(zip(sources, targets))
-        ]
-
-    for k in range(1, OWNERS):
-        for copy in copies(k, me):
-            copy.start()
-    for copy in local:
-        copy.wait()
-    for k in range(1, OWNERS):
-        for copy in copies(k, lax.rem(me + OWNERS - k, OWNERS)):
-            copy.wait()
-
-
-def exchange(arrays, collective_id):
-    count = len(arrays)
-    hbm = pl.BlockSpec(memory_space=pl.ANY)
-    return pl.pallas_call(
-        functools.partial(exchange_kernel, count),
-        out_shape=[jax.ShapeDtypeStruct(a.shape, a.dtype) for a in arrays],
-        in_specs=[hbm] * count,
-        out_specs=[hbm] * count,
-        scratch_shapes=[
-            pltpu.SemaphoreType.DMA((count, OWNERS)),
-            pltpu.SemaphoreType.DMA((count, OWNERS)),
-            pltpu.SemaphoreType.DMA((count,)),
-        ],
-        compiler_params=pltpu.CompilerParams(collective_id=collective_id, has_side_effects=True),
-        name="exchange%d" % collective_id,
-    )(*arrays)
-
-
-TO_POWERS = np.array([[1, 0, 0, 0], [-3, 3, 0, 0], [3, -6, 3, 0], [-1, 3, -3, 1]], np.float32)
-
-
-def power_matrix():
-    one = np.kron(np.eye(4, dtype=np.float32), np.kron(TO_POWERS, TO_POWERS))
-    pair = np.kron(np.eye(2, dtype=np.float32), one)
-    return np.concatenate([pair, pair], 1)
+def centre(c0, c1, c2, c3):
+    outer, inner = c0 + c3, c1 + c2
+    outer_diff, inner_diff = c3 - c0, c2 - c1
+    return (0.125 * outer + 0.375 * inner, 0.75 * (outer_diff + inner_diff),
+            1.5 * (outer - inner), outer_diff - 3.0 * inner_diff)
 
 
 def value_slope(a, t):
@@ -209,6 +155,7 @@
 
 
 def surface(load, u, v):
+    u, v = u - 0.5, v - 0.5
     point, along_u, along_v = [], [], []
     for c in range(4):
         values, slopes = [], []
@@ -243,99 +190,222 @@
     return surface(load, u, v)
 
 
-def project_kernel(recv_ref, net_hbm, powers_ref, main_ref, last_ref,
-                   net, index_v, odd, index_s, rows, control, last, sem):
-    loads = [
-        pltpu.make_async_copy(net_hbm.at[:, pl.ds(k * 128, 128)],
-                              net.at[pl.ds(k * PITCH, PATCH_DEV), :], sem.at[k])
-        for k in range(8)
+def project_kernel(out_ref, net_hbm, main_ref, last_ref,
+                   net, recv, index_v, index_a, index_b, rows_a, rows_b, turned, control_a, control_b,
+                   main, last, last_pair,
+                   net_sem, index_sem, own, send, arrive, back, home):
+    me = lax.axis_index("bulk")
+    barrier = pltpu.get_barrier_semaphore()
+    for k in range(1, OWNERS):
+        peer = lax.rem(me + k, OWNERS)
+        pl.semaphore_signal(barrier, inc=1, device_id={"bulk": peer}, device_id_type=MESH)
+    def net_copy(k):
+        return pltpu.make_async_copy(
+            net_hbm.at[:, pl.ds(pl.multiple_of(k * 128, 128), 128)],
+            net.at[pl.ds(pl.multiple_of(k * PITCH, 8), PATCH_DEV), :], net_sem.at[k])
+
+    for k in range(8):
+        net_copy(k).start()
+    first = pltpu.make_async_copy(out_ref.at[me], recv.at[pl.ds(0, SLOT), :], own.at[0])
+    first.start()
+    last[...] = jnp.zeros_like(last)
+    pl.semaphore_wait(barrier, OWNERS - 1)
+
+    def outward(k):
+        peer = lax.rem(me + k, OWNERS)
+        return pltpu.make_async_remote_copy(
+            src_ref=out_ref.at[peer],
+            dst_ref=recv.at[pl.ds(pl.multiple_of(k * SLOT, 8), SLOT), :],
+            send_sem=send.at[k], recv_sem=arrive.at[k],
+            device_id={"bulk": peer}, device_id_type=MESH,
+        )
+
+    def homeward(k, owner):
+        peer = lax.rem(me + OWNERS - k, OWNERS)
+        return [
+            pltpu.make_async_remote_copy(
+                src_ref=s.at[pl.ds(pl.multiple_of(k * n, 8), n), :],
+                dst_ref=t.at[pl.ds(pl.multiple_of(owner * n, 8), n), :],
+                send_sem=back.at[i, k], recv_sem=home.at[i, k],
+                device_id={"bulk": peer}, device_id_type=MESH,
+            )
+            for i, (s, t, n) in enumerate(((main, main_ref, SLOT), (last, last_ref, 24)))
+        ]
+
+    stay = [
+        pltpu.make_async_copy(main.at[pl.ds(0, SLOT), :],
+                              main_ref.at[pl.ds(pl.multiple_of(me * SLOT, 8), SLOT), :], own.at[1]),
+        pltpu.make_async_copy(last.at[pl.ds(0, 24), :],
+                              last_ref.at[pl.ds(pl.multiple_of(me * 24, 8), 24), :], own.at[2]),
     ]
-    for copy in loads:
-        copy.start()
-
-    def prepare(b, carry):
-        code = recv_ref[pl.ds(b * 64 + 5, 8, stride=8), :].astype(I32)
-        index_v[pl.ds(b * 8, 8), :] = code >> 1
-        odd[pl.ds(b * 8, 8), :] = code & 1
+
+    def start_outward(k, carry):
+        outward(k).start()
         return carry
 
-    lax.fori_loop(0, GROUPS // BATCH, prepare, 0)
-    copy = pltpu.make_async_copy(index_v, index_s, sem.at[8])
-    copy.start()
-    for each in loads:
-        each.wait()
-    copy.wait()
-
-    def body(b, carry):
-        for g in range(BATCH):
+    lax.fori_loop(1, OWNERS, start_outward, 0)
+
+    def swap_halves(k, carry):
+        net_copy(k).wait()
+        for t in range(PITCH // 8):
+            at = pl.multiple_of(k * PITCH + t * 8, 8)
+            net[pl.ds(pl.multiple_of(at + TABLE, 8), 8), :] = pltpu.roll(net[pl.ds(at, 8), :], 64, axis=1)
+        return carry
+
+    lax.fori_loop(0, 8, swap_halves, 0)
+    row, lane = iota((8, 128), 0), iota((8, 128), 1)
+    masks = [[(row == s) & (lane < 64), (row == s) & (lane >= 64)] for s in range(8)]
+
+    def prepare(m):
+        for i in range(PAIR_BATCHES):
+            b = m * PAIR_BATCHES + i
+            code = recv[pl.ds(b * 64 + 5, 8, stride=8), :].astype(I32)
+            code = jnp.clip(code, 0, 2 * TABLE - 1)
+            swapped = jnp.where(code >= TABLE, code - TABLE, code + TABLE)
+            index_v[b] = jnp.where((row & 1) == 1, swapped, code)
+
+    def index_copy(b, half):
+        return pltpu.make_async_copy(index_v.at[b], (index_a, index_b)[half], index_sem.at[half])
+
+    def gather(index, rows):
+        for h in range(4):
             for t in range(16):
-                parts = [net[pl.ds(index_s[b * 8 + g, t * 8 + s], 1), :] for s in range(8)]
-                rows[pl.ds(g * 128 + t * 8, 8), :] = jnp.concatenate(parts, 0)
+                x = None
+                for s in range(8):
+                    for q in range(2):
+                        w = net[pl.ds(index[2 * h + q, t * 8 + s], 8, stride=0), :]
+                        x = w if x is None else jnp.where(masks[s][q], w, x)
+                rows[pl.ds(h * 128 + t * 8, 8), :] = x
+
+    def to_powers(rows, control):
         for h in range(4):
-            x = rows[pl.ds(h * 256, 256), :]
-            high = x.astype(BF16)
-            low = (x - high.astype(F32)).astype(BF16)
-            flat = lax.dot_general(powers_ref[...], jnp.concatenate([high, low], 1),
-                                   (((1,), (1,)), ((), ())), preferred_element_type=F32)
-            for q in range(2):
-                which = odd[pl.ds(b * 8 + h * 2 + q, 1), :]
-                part = flat[:, q * 128:(q + 1) * 128]
-                control[pl.ds((h * 2 + q) * 64, 64), :] = jnp.where(which == 1, part[64:], part[:64])
+            turned[pl.ds(h * 128, 128), :] = rows[pl.ds(h * 128, 128), :].T
+        for c in range(4):
+            along = [
+                centre(*[turned[pl.ds(c * 16 + i * 4 + j, 8, stride=64), :] for i in range(4)])
+                for j in range(4)
+            ]
+            for i in range(4):
+                for j, x in enumerate(centre(*[along[j][i] for j in range(4)])):
+                    control[c * 16 + i * 4 + j] = x
+
+    first.wait()
+    outward(1).wait_recv()
+    prepare(0)
+    for half, (index, rows) in enumerate(((index_a, rows_a), (index_b, rows_b))):
+        index_copy(half, half).start()
+        index_copy(half, half).wait()
+        gather(index, rows)
+        index_copy(half + 2, half).start()
+    to_powers(rows_a, control_a)
+
+    def batch(b, half):
+        index, rows, other, control, following = (
+            (index_a, rows_a, rows_b, control_a, control_b),
+            (index_b, rows_b, rows_a, control_b, control_a),
+        )[half]
+        m = lax.div(b, PAIR_BATCHES)
+        i = b - m * PAIR_BATCHES
+        index_copy(0, half).wait()
+        gather(index, rows)
+        to_powers(other, following)
 
         def load(k):
-            return control[pl.ds(k, 8, stride=64), :]
+            return control[k]
 
         def value(k):
-            return recv_ref[pl.ds(b * 64 + k, 8, stride=8), :]
+            return recv[pl.ds(b * 64 + k, 8, stride=8), :]
 
         p, su, sv = project(load, [value(0), value(1), value(2)], value(3), value(4))
         for k, x in enumerate((p + su + sv)[:8]):
-            main_ref[pl.ds(b * 64 + k, 8, stride=8), :] = x
-        last[pl.ds(b * 8, 8), :] = sv[2]
+            main[pl.ds(b * 64 + k, 8, stride=8), :] = x
+        last_pair[pl.ds(pl.multiple_of(i * 8, 8), 8), :] = sv[2]
+
+        @pl.when((i == 1) & (m < OWNERS // 2 - 1))
+        def _():
+            outward(2 * m + 2).wait_recv()
+            outward(2 * m + 3).wait_recv()
+            prepare(m + 1)
+
+        index_copy(jnp.minimum(b + 4, BATCHES - 1), half).start()
+
+        @pl.when(i == PAIR_BATCHES - 1)
+        def _():
+            for h in range(2):
+                at = pl.multiple_of((2 * m + h) * 24, 8)
+                last[pl.ds(at, TILES), :] = last_pair[h * TILES:(h + 1) * TILES, :]
+
+            @pl.when(m == 0)
+            def _():
+                for copy in stay:
+                    copy.start()
+
+            @pl.when(m > 0)
+            def _():
+                for copy in homeward(2 * m, me):
+                    copy.start()
+
+            for copy in homeward(2 * m + 1, me):
+                copy.start()
+
+    def two(q, carry):
+        batch(2 * q, 0)
+        batch(2 * q + 1, 1)
         return carry
 
-    lax.fori_loop(0, GROUPS // BATCH, body, 0)
-    for o in range(OWNERS):
-        last_ref[o, 0:TILES, :] = last[pl.ds(o * TILES, TILES), :]
-        last_ref[o, TILES:24, :] = jnp.zeros((24 - TILES, 128), F32)
-
-
-def place_nodes(received, net):
+    lax.fori_loop(0, BATCHES // 2, two, 0)
+    for half in range(2):
+        index_copy(0, half).wait()
+    for copy in stay:
+        copy.wait()
+
+    def finish(k, carry):
+        outward(k).wait_send()
+        for copy in homeward(k, lax.rem(me + k, OWNERS)):
+            copy.wait()
+        return carry
+
+    lax.fori_loop(1, OWNERS, finish, 0)
+
+
+def place_nodes(outgoing, net):
     vmem = pl.BlockSpec(memory_space=pltpu.VMEM)
+    dma = pltpu.SemaphoreType.DMA
     return pl.pallas_call(
         project_kernel,
         out_shape=[
-            jax.ShapeDtypeStruct((GROUPS * 8, 128), F32),
-            jax.ShapeDtypeStruct((OWNERS, 24, 128), F32),
+            jax.ShapeDtypeStruct((GROUPS * 8 + 24, 128), F32),
+            jax.ShapeDtypeStruct((OWNERS * 24, 128), F32),
         ],
-        in_specs=[vmem, pl.BlockSpec(memory_space=pl.ANY), vmem],
+        in_specs=[vmem, pl.BlockSpec(memory_space=pl.ANY)],
         out_specs=[vmem] * 2,
         scratch_shapes=[
-            pltpu.VMEM((8 * PITCH, 128), F32),
-            pltpu.VMEM((GROUPS, 128), I32),
-            pltpu.VMEM((GROUPS, 128), I32),
-            pltpu.SMEM((GROUPS, 128), I32),
-            pltpu.VMEM((BATCH * 128, 128), F32),
+            pltpu.VMEM((2 * TABLE, 128), F32),
+            pltpu.VMEM((GROUPS * 8 + 64, 128), F32),
+            pltpu.VMEM((BATCHES, 8, 128), I32),
+            pltpu.SMEM((8, 128), I32),
+            pltpu.SMEM((8, 128), I32),
             pltpu.VMEM((BATCH * 64, 128), F32),
-            pltpu.VMEM((GROUPS, 128), F32),
-            pltpu.SemaphoreType.DMA((9,)),
+            pltpu.VMEM((BATCH * 64, 128), F32),
+            pltpu.VMEM((BATCH * 64 + 64, 128), F32),
+            pltpu.VMEM((64, 8, 128), F32),
+            pltpu.VMEM((64, 8, 128), F32),
+            pltpu.VMEM((GROUPS * 8 + 64, 128), F32),
+            pltpu.VMEM((OWNERS * 24, 128), F32),
+            pltpu.VMEM((2 * TILES, 128), F32),
+            dma((8,)), dma((2,)), dma((3,)),
+            dma((OWNERS,)), dma((OWNERS,)), dma((2, OWNERS)), dma((2, OWNERS)),
         ],
-        compiler_params=pltpu.CompilerParams(vmem_limit_bytes=48 << 20),
+        compiler_params=pltpu.CompilerParams(
+            collective_id=1, has_side_effects=True, vmem_limit_bytes=48 << 20),
         name="project",
-    )(received.reshape(GROUPS * 8, 128), net, jnp.asarray(power_matrix(), BF16))
-
-
-def collect_kernel(main_hbm, last_hbm, place_ref, table_hbm, out_ref, main, last, table_s, sem):
-    copies = [
-        pltpu.make_async_copy(main_hbm, main.at[pl.ds(0, GROUPS * 8), :], sem.at[0]),
-        pltpu.make_async_copy(last_hbm, last.at[pl.ds(0, OWNERS * 24), :], sem.at[1]),
-        pltpu.make_async_copy(table_hbm, table_s, sem.at[2]),
-    ]
-    for copy in copies:
-        copy.start()
-    main[pl.ds(GROUPS * 8, 24), :] = jnp.zeros((24, 128), F32)
-    for copy in copies:
-        copy.wait()
+    )(outgoing, net)
+
+
+def collect_kernel(main, last, place_ref, table_hbm, out_ref, table_s, sem):
+    copy = pltpu.make_async_copy(table_hbm, table_s, sem)
+    copy.start()
+    copy.wait()
     lane = iota((8, 128), 1)
 
     def body(j, carry):
@@ -372,24 +442,17 @@
     return pl.pallas_call(
         collect_kernel,
         out_shape=jax.ShapeDtypeStruct((9, 16384), F32),
-        in_specs=[hbm, hbm, vmem, hbm],
+        in_specs=[vmem, vmem, vmem, hbm],
         out_specs=vmem,
-        scratch_shapes=[
-            pltpu.VMEM((GROUPS * 8 + 24, 128), F32),
-            pltpu.VMEM((OWNERS * 24, 128), F32),
-            pltpu.SMEM((64, 128), I32),
-            pltpu.SemaphoreType.DMA((3,)),
-        ],
+        scratch_shapes=[pltpu.SMEM((64, 128), I32), pltpu.SemaphoreType.DMA],
         compiler_params=pltpu.CompilerParams(vmem_limit_bytes=32 << 20),
         name="collect",
-    )(main.reshape(GROUPS * 8, 128), last.reshape(OWNERS * 24, 128), place, table)
+    )(main, last, place, table)
 
 
 def body(node_patch, node_span, start_grid, target, net):
     outgoing, place, table = dispatch(node_patch, node_span, start_grid, target)
-    (received,) = exchange([outgoing], 1)
-    main, last = place_nodes(received, net)
-    main, last = exchange([main.reshape(OWNERS, TILES * 8, 128), last], 2)
+    main, last = place_nodes(outgoing, net)
     return collect(main, last, place, table)
 
 

time: 161 us -> 117 us (0.73); the launches traced: 159 us -> 117 us
  Pallas kernels: 149 us -> 113 us
  local copies, waits for them, and re-layouts: 9.9 us -> 3.53 us
    pallas_call x2 -> x0, Pallas kernels: 49.9 us -> none  [exchange(): pl.pallas_call(functools.partial(exchange_kernel, count), out_shape=[jax....]
    pallas_call x1, Pallas kernels: 57 us -> 71.7 us  [place_nodes(): pl.pallas_call(project_kernel, out_shape=[jax.ShapeDtypeStruct((GROUPS *...]
    unnamed x22 -> x8, local copies, waits for them, and re-layouts: 9.9 us -> 3.53 us
where the time goes in v2:
time: 117 us
  Pallas kernels  113 us (97%)
  local copies, waits for them, and re-layouts  3.53 us (3%)
    pallas_call x1, Pallas kernels, place_nodes(): pl.pallas_call(project_kernel, out_shape=[jax.ShapeDtypeStruct((GROUPS *...  71.7 us
    pallas_call x1, Pallas kernels, dispatch(): pl.pallas_call(dispatch_kernel, out_shape=[jax.ShapeDtypeStruct((OWNERS,...  22.8 us
    pallas_call x1, Pallas kernels, collect(): pl.pallas_call(collect_kernel, out_shape=jax.ShapeDtypeStruct((9, 16384),...  18.9 us
    unnamed x8, local copies, waits for them, and re-layouts  3.53 us

profile of v2, /device:TPU:36, one launch (start us, length us, event | category | flops | bytes accessed | tf_op | source)
XLA Modules:
  0.0 117.0 jit_solution(7334249044870964309)
XLA Ops:
  0.0 0.0 copy-start
  0.0 0.9 copy-done
  1.0 0.0 copy-start.1
  1.0 0.9 copy-done.1
  1.9 0.0 copy-start.2
  1.9 0.8 copy-done.2
  2.7 0.0 copy-start.3
  2.7 0.8 copy-done.3
  3.5 22.8 %dispatch.1 = (f32[16,160,128]{2,1,0:T(8,128)S(1)}, f32[128,128]{1,0:T(8,128)S(1)}, s32[64,128]{1,0:T(8,128)S(1)}) custom-call(s32[128,128]{1,0:T(8,128)S(1)} %bitcast.2, s32[128,128]{1,0:T(8,128)S(1)} %bitcast.3, s32[2,16384]{1,0:T(2,128)S(1)} %copy-done.1, f32[3,16384]{1,0:T(4,128)S(1)} %copy-done), custom_call_target="tpu_custom_call" | custom-call | tf_op jit(solution)/shard_map/dispatch/pallas_call | solution.py:118
  26.3 71.7 %project.1 = (f32[2584,128]{1,0:T(8,128)S(1)}, f32[384,128]{1,0:T(8,128)S(1)}) custom-call(f32[16,160,128]{2,1,0:T(8,128)S(1)} %get-tuple-element.10.out_ref, f32[2500,1024]{1,0:T(8,128)} %net_hbm.1), custom_call_target="tpu_custom_call" | custom-call | tf_op jit(solution)/shard_map/project/pallas_call | solution.py:374
  98.0 18.9 %collect.1 = f32[9,16384]{1,0:T(8,128)} custom-call(f32[2584,128]{1,0:T(8,128)S(1)} %get-tuple-element.11.main, f32[384,128]{1,0:T(8,128)S(1)} %get-tuple-element.12.last, f32[128,128]{1,0:T(8,128)S(1)} %get-tuple-element.13.place_ref, s32[64,128]{1,0:T(8,128)S(1)} %get-tuple-element.14.table_hbm), custom_call_target="tpu_custom_call" | custom-call | tf_op jit(solution)/shard_map/collect/pallas_call | solution.py:442
Async XLA Ops:
  0.0 0.9 copy-start
  1.0 0.9 copy-start.1
  1.9 0.8 copy-start.2
  2.7 0.8 copy-start.3

commit v3 on v2

--- a/solution.py
+++ b/solution.py
@@ -22,6 +22,7 @@
 GROUPS = OWNERS * TILES
 MARGIN = 3
 BATCH = 8
+TURN = 72
 SLOT = TILES * 8
 PAIR_BATCHES = 2 * TILES // BATCH
 BATCHES = GROUPS // BATCH
@@ -44,8 +45,19 @@
     return jnp.where(iota((256, 256), 0).astype(F32) == place, 1.0, 0.0).astype(BF16)
 
 
-def dispatch_kernel(patch_ref, span_ref, start_ref, target_ref, out_ref, place_ref, table_ref,
-                    code_ref, values, stage, table_v, table_s, sem):
+def dispatch_kernel(patch_hbm, span_hbm, start_hbm, target_hbm, out_ref, place_ref, table_ref,
+                    patch_ref, span_ref, start_ref, code_ref, values, ordered, stage, table_v, table_s, sem):
+    copies = [
+        pltpu.make_async_copy(patch_hbm, patch_ref, sem.at[0]),
+        pltpu.make_async_copy(span_hbm, span_ref, sem.at[1]),
+        pltpu.make_async_copy(start_hbm, start_ref, sem.at[2]),
+        pltpu.make_async_copy(target_hbm, values.at[pl.ds(0, 3), :], sem.at[3]),
+    ]
+    for copy in copies:
+        copy.start()
+    stage[...] = jnp.zeros_like(stage)
+    copies[0].wait()
+    copies[1].wait()
     patch = patch_ref[...]
     span = span_ref[...]
     owner = ((patch.astype(F32) + 0.5) * (1.0 / PATCH_DEV)).astype(I32)
@@ -67,48 +79,59 @@
         place += mine * jnp.concatenate([earlier[:64] + begin, earlier[64:] + total[:64] + begin], 0)
         first = begin.astype(I32)
         offset = base & 127
-        columns = ((offset - first) & 255, offset, base >> 7, offset + count.astype(I32),
-                   first, (first - offset) & 255)
+        columns = (offset - first, offset, base >> 7, offset + count.astype(I32), first)
         for k, column in enumerate(columns):
             table = jnp.where(lane == k * OWNERS + o, column, table)
         begin = begin + count
     place_ref[...] = place
     table_v[...] = table
     table_ref[...] = table
-    copy = pltpu.make_async_copy(table_v, table_s, sem)
+    copy = pltpu.make_async_copy(table_v, table_s, sem.at[4])
     copy.start()
-    values[0:3, :] = target_ref[...]
+    copies[2].wait()
+    copies[3].wait()
     values[3:5, :] = (start_ref[...].astype(F32) + 0.5) * (1.0 / LEVELS)
     values[5:8, :] = jnp.zeros((3, values.shape[1]), F32)
-    stage[...] = jnp.zeros_like(stage)
-    copy.wait()
     row = iota((8, 128), 0)
     lane = iota((8, 128), 1)
 
-    def body(j, current):
-        halves = []
-        for h in range(2):
-            r = j + 64 * h
-            x = values[:, pl.ds(pl.multiple_of(r * 128, 128), 128)]
-            halves.append(jnp.where(row == 5, code_ref[pl.ds(r, 8, stride=0), :], x))
-        x = split3(jnp.concatenate(halves, 1))
-        y = lax.dot_general(x, block_permutation(place_ref, j), (((1,), (1,)), ((), ())),
-                            preferred_element_type=F32)
-        y = y[0:8] + y[8:16] + y[16:24]
-        following = []
-        for o in range(OWNERS):
-            rolled = pltpu.roll(y, table_s[j, o], axis=1)
-            left, right = rolled[:, :128], rolled[:, 128:]
-            offset, tile, end = table_s[j, 16 + o], table_s[j, 32 + o], table_s[j, 48 + o]
-            merged = jnp.where(lane >= offset, left, current[o])
-            at = pl.multiple_of((o * (TILES + MARGIN) + tile) * 8, 8)
-            stage[pl.ds(at, 8), :] = merged
-            stage[pl.ds(at + 8, 8), :] = right
-            stage[pl.ds(at + 16, 8), :] = left
-            following.append(jnp.where(end < 128, merged, jnp.where(end < 256, right, left)))
-        return tuple(following)
-
-    lax.fori_loop(0, 64, body, tuple(jnp.zeros((8, 128), F32) for _ in range(OWNERS)))
+    def order(i, carry):
+        for step in range(4):
+            j = i * 4 + step
+            halves = []
+            for h in range(2):
+                r = j + 64 * h
+                x = values[:, pl.ds(pl.multiple_of(r * 128, 128), 128)]
+                halves.append(jnp.where(row == 5, code_ref[pl.ds(r, 8, stride=0), :], x))
+            x = split3(jnp.concatenate(halves, 1))
+            y = lax.dot_general(x, block_permutation(place_ref, j), (((1,), (1,)), ((), ())),
+                                preferred_element_type=F32)
+            ordered[j] = y[0:8] + y[8:16] + y[16:24]
+        return carry
+
+    lax.fori_loop(0, 16, order, 0)
+    copy.wait()
+
+    def append(i, current):
+        current = list(current)
+        for step in range(2):
+            j = i * 2 + step
+            y0, y1 = ordered[j, :, 0:128], ordered[j, :, 128:256]
+            for o in range(OWNERS):
+                move, offset = table_s[j, o], table_s[j, 16 + o]
+                tile, end = table_s[j, 32 + o], table_s[j, 48 + o]
+                r0 = pltpu.roll(y0, move & 127, axis=1)
+                r1 = pltpu.roll(y1, move & 127, axis=1)
+                second = jnp.where(lane >= move, r1, r0)
+                merged = jnp.where(lane >= offset, jnp.where(lane >= move + 128, r1, r0), current[o])
+                at = pl.multiple_of((o * (TILES + MARGIN) + tile) * 8, 8)
+                stage[pl.ds(at, 8), :] = merged
+                stage[pl.ds(at + 8, 8), :] = second
+                stage[pl.ds(at + 16, 8), :] = r1
+                current[o] = jnp.where(end < 128, merged, jnp.where(end < 256, second, r1))
+        return tuple(current)
+
+    lax.fori_loop(0, 32, append, tuple(jnp.zeros((8, 128), F32) for _ in range(OWNERS)))
     for o in range(OWNERS):
         out_ref[o] = stage[pl.ds(o * (TILES + MARGIN) * 8, TILES * 8), :]
 
@@ -122,17 +145,21 @@
             jax.ShapeDtypeStruct((128, 128), F32),
             jax.ShapeDtypeStruct((64, 128), I32),
         ],
-        in_specs=[vmem] * 4,
+        in_specs=[pl.BlockSpec(memory_space=pl.ANY)] * 4,
         out_specs=[vmem] * 3,
         scratch_shapes=[
+            pltpu.VMEM((128, 128), I32),
+            pltpu.VMEM((128, 128), I32),
+            pltpu.VMEM((2, 16384), I32),
             pltpu.VMEM((128, 128), F32),
             pltpu.VMEM((8, 16384), F32),
+            pltpu.VMEM((64, 8, 256), F32),
             pltpu.VMEM((OWNERS * (TILES + MARGIN) * 8, 128), F32),
             pltpu.VMEM((64, 128), I32),
             pltpu.SMEM((64, 128), I32),
-            pltpu.SemaphoreType.DMA,
+            pltpu.SemaphoreType.DMA((5,)),
         ],
-        compiler_params=pltpu.CompilerParams(vmem_limit_bytes=32 << 20),
+        compiler_params=pltpu.CompilerParams(vmem_limit_bytes=62 << 20),
         name="dispatch",
     )(patch.reshape(128, 128), span.reshape(128, 128), start, target)
 
@@ -279,10 +306,12 @@
 
     def to_powers(rows, control):
         for h in range(4):
-            turned[pl.ds(h * 128, 128), :] = rows[pl.ds(h * 128, 128), :].T
+            both = rows[pl.ds(h * 128, 128), :].T
+            turned[pl.ds(2 * h * TURN, 64), :] = both[:64]
+            turned[pl.ds((2 * h + 1) * TURN, 64), :] = both[64:]
         for c in range(4):
             along = [
-                centre(*[turned[pl.ds(c * 16 + i * 4 + j, 8, stride=64), :] for i in range(4)])
+                centre(*[turned[pl.ds(c * 16 + i * 4 + j, 8, stride=TURN), :] for i in range(4)])
                 for j in range(4)
             ]
             for i in range(4):
@@ -387,7 +416,7 @@
             pltpu.SMEM((8, 128), I32),
             pltpu.VMEM((BATCH * 64, 128), F32),
             pltpu.VMEM((BATCH * 64, 128), F32),
-            pltpu.VMEM((BATCH * 64 + 64, 128), F32),
+            pltpu.VMEM((BATCH * TURN + 64, 128), F32),
             pltpu.VMEM((64, 8, 128), F32),
             pltpu.VMEM((64, 8, 128), F32),
             pltpu.VMEM((GROUPS * 8 + 64, 128), F32),
@@ -402,38 +431,52 @@
     )(outgoing, net)
 
 
-def collect_kernel(main, last, place_ref, table_hbm, out_ref, table_s, sem):
+def collect_kernel(main, last, place_ref, table_hbm, out_ref, ordered, table_s, sem):
     copy = pltpu.make_async_copy(table_hbm, table_s, sem)
     copy.start()
     copy.wait()
     lane = iota((8, 128), 1)
 
-    def body(j, carry):
-        acc = [jnp.zeros((8, 128), F32) for _ in range(4)]
-        for o in range(OWNERS):
-            offset, tile = table_s[j, 16 + o], table_s[j, 32 + o]
-            first, shift = table_s[j, 64 + o], table_s[j, 80 + o]
-            keep, low, high = lane >= offset, lane >= first, lane >= first - 128
-            at = pl.multiple_of((o * TILES + tile) * 8, 8)
-            row = o * 24 + tile
-            windows = (
-                [main[pl.ds(at + 8 * i, 8), :] for i in range(3)],
-                [last[pl.ds(row + i, 8, stride=0), :] for i in range(3)],
-            )
-            for i, (w0, w1, w2) in enumerate(windows):
-                x = jnp.concatenate([jnp.where(keep, w0, w2), w1], 1)
-                x = pltpu.roll(x, shift, axis=1)
-                acc[2 * i] = jnp.where(low, x[:, :128], acc[2 * i])
-                acc[2 * i + 1] = jnp.where(high, x[:, 128:], acc[2 * i + 1])
-        x = jnp.concatenate([jnp.concatenate(acc[:2], 1), jnp.concatenate(acc[2:], 1)], 0)
-        y = jnp.dot(split3(x), block_permutation(place_ref, j), preferred_element_type=F32)
-        y = y[0:16] + y[16:32] + y[32:48]
-        for h in range(2):
-            at = pl.multiple_of((j + 64 * h) * 128, 128)
-            out_ref[:, pl.ds(at, 128)] = y[0:9, h * 128:(h + 1) * 128]
-        return carry
-
-    lax.fori_loop(0, 64, body, 0)
+    def assemble(i, carry):
+        for step in range(2):
+            j = i * 2 + step
+            acc = [jnp.zeros((8, 128), F32) for _ in range(4)]
+            for o in range(OWNERS):
+                move, offset = table_s[j, o], table_s[j, 16 + o]
+                tile, first = table_s[j, 32 + o], table_s[j, 64 + o]
+                at = pl.multiple_of((o * TILES + tile) * 8, 8)
+                at_last = o * 24 + tile
+                keep = lane >= offset
+                in_low, in_high = lane >= first, lane >= first - 128
+                from_low = lane >= 128 - move
+                from_high = (lane >= -move) & (lane < 128 - move)
+                windows = (
+                    [main[pl.ds(at + 8 * k, 8), :] for k in range(3)],
+                    [last[pl.ds(at_last + k, 8, stride=0), :] for k in range(3)],
+                )
+                for k, (w0, w1, w2) in enumerate(windows):
+                    r0 = pltpu.roll(jnp.where(keep, w0, w2), (-move) & 127, axis=1)
+                    r1 = pltpu.roll(w1, (-move) & 127, axis=1)
+                    acc[2 * k] = jnp.where(in_low, jnp.where(from_low, r1, r0), acc[2 * k])
+                    acc[2 * k + 1] = jnp.where(in_high, jnp.where(from_high, r1, r0), acc[2 * k + 1])
+            for k in range(2):
+                ordered[j, 8 * k:8 * k + 8, 0:128] = acc[2 * k]
+                ordered[j, 8 * k:8 * k + 8, 128:256] = acc[2 * k + 1]
+        return carry
+
+    lax.fori_loop(0, 32, assemble, 0)
+
+    def spread(i, carry):
+        for step in range(4):
+            j = i * 4 + step
+            y = jnp.dot(split3(ordered[j]), block_permutation(place_ref, j), preferred_element_type=F32)
+            y = y[0:16] + y[16:32] + y[32:48]
+            for h in range(2):
+                at = pl.multiple_of((j + 64 * h) * 128, 128)
+                out_ref[:, pl.ds(at, 128)] = y[0:9, h * 128:(h + 1) * 128]
+        return carry
+
+    lax.fori_loop(0, 16, spread, 0)
 
 
 def collect(main, last, place, table):
@@ -444,7 +487,7 @@
         out_shape=jax.ShapeDtypeStruct((9, 16384), F32),
         in_specs=[vmem, vmem, vmem, hbm],
         out_specs=vmem,
-        scratch_shapes=[pltpu.SMEM((64, 128), I32), pltpu.SemaphoreType.DMA],
+        scratch_shapes=[pltpu.VMEM((64, 16, 256), F32), pltpu.SMEM((64, 128), I32), pltpu.SemaphoreType.DMA],
         compiler_params=pltpu.CompilerParams(vmem_limit_bytes=32 << 20),
         name="collect",
     )(main, last, place, table)

time: 117 us -> 97.1 us (0.83)
  Pallas kernels: 113 us -> 95.5 us
  local copies, waits for them, and re-layouts: 3.53 us -> 1.32 us
    pallas_call x1, Pallas kernels: 22.8 us -> 15.6 us  [dispatch(): pl.pallas_call(dispatch_kernel, out_shape=[jax.ShapeDtypeStruct((OWNERS,...]
    pallas_call x1, Pallas kernels: 18.9 us -> 12 us  [collect(): pl.pallas_call(collect_kernel, out_shape=jax.ShapeDtypeStruct((9, 16384),...]
    pallas_call x1, Pallas kernels: 71.7 us -> 67.9 us  [place_nodes(): pl.pallas_call(project_kernel, out_shape=[jax.ShapeDtypeStruct((GROUPS *...]
    unnamed x8 -> x6, local copies, waits for them, and re-layouts: 3.53 us -> 1.32 us
where the time goes in v3:
time: 97.1 us; the launch traced here: 96.9 us
  Pallas kernels  95.5 us (98%)
  local copies, waits for them, and re-layouts  1.32 us (1%)
    pallas_call x1, Pallas kernels, place_nodes(): pl.pallas_call(project_kernel, out_shape=[jax.ShapeDtypeStruct((GROUPS *...  67.9 us
    pallas_call x1, Pallas kernels, dispatch(): pl.pallas_call(dispatch_kernel, out_shape=[jax.ShapeDtypeStruct((OWNERS,...  15.6 us
    pallas_call x1, Pallas kernels, collect(): pl.pallas_call(collect_kernel, out_shape=jax.ShapeDtypeStruct((9, 16384),...  12 us

profile of v3, /device:TPU:36, one launch (start us, length us, event | category | flops | bytes accessed | tf_op | source)
XLA Modules:
  0.0 96.9 jit_solution(7563992772288342036)
XLA Ops:
  0.0 15.6 %dispatch.1 = (f32[16,160,128]{2,1,0:T(8,128)}, f32[128,128]{1,0:T(8,128)}, s32[64,128]{1,0:T(8,128)}) custom-call(s32[128,128]{1,0:T(8,128)} %bitcast.2, s32[128,128]{1,0:T(8,128)} %bitcast.3, s32[2,16384]{1,0:T(2,128)} %start_hbm.1, f32[3,16384]{1,0:T(4,128)} %target_hbm.1), custom_call_target="tpu_custom_call" | custom-call | tf_op jit(solution)/shard_map/dispatch/pallas_call | solution.py:141
  15.6 0.0 copy-start
  15.6 1.3 %copy-done = f32[16,160,128]{2,1,0:T(8,128)S(1)} copy-done((f32[16,160,128]{2,1,0:T(8,128)S(1)}, f32[16,160,128]{2,1,0:T(8,128)}, u32[]{:S(2)}) %copy-start) | copy-done | bytes 1310744
  16.9 0.0 copy-start.1
  17.0 0.0 copy-start.2
  17.0 67.9 %project.1 = (f32[2584,128]{1,0:T(8,128)S(1)}, f32[384,128]{1,0:T(8,128)S(1)}) custom-call(f32[16,160,128]{2,1,0:T(8,128)S(1)} %copy-done, f32[2500,1024]{1,0:T(8,128)} %net_hbm.1), custom_call_target="tpu_custom_call" | custom-call | tf_op jit(solution)/shard_map/project/pallas_call | solution.py:403
  84.9 0.0 copy-done.1
  84.9 0.0 copy-done.2
  84.9 12.0 %collect.1 = f32[9,16384]{1,0:T(8,128)} custom-call(f32[2584,128]{1,0:T(8,128)S(1)} %get-tuple-element.11.main, f32[384,128]{1,0:T(8,128)S(1)} %get-tuple-element.12.last, f32[128,128]{1,0:T(8,128)S(1)} %copy-done.1, s32[64,128]{1,0:T(8,128)S(1)} %copy-done.2), custom_call_target="tpu_custom_call" | custom-call | tf_op jit(solution)/shard_map/collect/pallas_call | solution.py:485
Async XLA Ops:
  15.6 1.3 %copy-start = (f32[16,160,128]{2,1,0:T(8,128)S(1)}, f32[16,160,128]{2,1,0:T(8,128)}, u32[]{:S(2)}) copy-start(f32[16,160,128]{2,1,0:T(8,128)} %get-tuple-element.10.out_ref) | copy-start | bytes 3932164
  16.9 67.9 %copy-start.1 = (f32[128,128]{1,0:T(8,128)S(1)}, f32[128,128]{1,0:T(8,128)}, u32[]{:S(2)}) copy-start(f32[128,128]{1,0:T(8,128)} %get-tuple-element.13.place_ref) | copy-start | bytes 196612
  17.0 67.9 %copy-start.2 = (s32[64,128]{1,0:T(8,128)S(1)}, s32[64,128]{1,0:T(8,128)}, u32[]{:S(2)}) copy-start(s32[64,128]{1,0:T(8,128)} %get-tuple-element.14.table_hbm) | copy-start | bytes 98308

commit v4 on v3

--- a/solution.py
+++ b/solution.py
@@ -21,6 +21,7 @@
 TILES = 20
 GROUPS = OWNERS * TILES
 MARGIN = 3
+STEPS = 4
 BATCH = 8
 TURN = 72
 SLOT = TILES * 8
@@ -68,21 +69,25 @@
     lower = (iota((64, 64), 0) > iota((64, 64), 1)).astype(F32).astype(BF16)
     lane = iota((64, 128), 1)
     begin = jnp.zeros((64, 128), F32)
+    counts = jnp.zeros((64, 128), F32)
     place = jnp.zeros((128, 128), F32)
-    table = jnp.zeros((64, 128), I32)
     for o in range(OWNERS):
-        mine = (owner == o).astype(F32)
-        both = jnp.dot(mine.astype(BF16), upper, preferred_element_type=F32)
+        mine = owner == o
+        both = jnp.dot(mine.astype(F32).astype(BF16), upper, preferred_element_type=F32)
         earlier, total = both[:, :128], both[:, 128:]
         count = total[:64] + total[64:]
-        base = jnp.dot(lower, count.astype(BF16), preferred_element_type=F32).astype(I32)
-        place += mine * jnp.concatenate([earlier[:64] + begin, earlier[64:] + total[:64] + begin], 0)
-        first = begin.astype(I32)
-        offset = base & 127
-        columns = (offset - first, offset, base >> 7, offset + count.astype(I32), first)
-        for k, column in enumerate(columns):
-            table = jnp.where(lane == k * OWNERS + o, column, table)
+        place = jnp.where(
+            mine, jnp.concatenate([earlier[:64] + begin, earlier[64:] + (total[:64] + begin)], 0), place)
+        counts = jnp.where(lane == o, count, counts)
         begin = begin + count
+    narrow = counts.astype(BF16)
+    base = jnp.dot(lower, narrow, preferred_element_type=F32).astype(I32)
+    first = jnp.dot(narrow, upper[:, :128], preferred_element_type=F32).astype(I32)
+    offset = base & 127
+    columns = (offset - first, offset, base >> 7, offset + counts.astype(I32), first)
+    table = columns[0]
+    for k, column in enumerate(columns[1:], 1):
+        table = jnp.where(lane >= k * OWNERS, pltpu.roll(column, k * OWNERS, axis=1), table)
     place_ref[...] = place
     table_v[...] = table
     table_ref[...] = table
@@ -95,28 +100,30 @@
     row = iota((8, 128), 0)
     lane = iota((8, 128), 1)
 
-    def order(i, carry):
-        for step in range(4):
-            j = i * 4 + step
-            halves = []
-            for h in range(2):
-                r = j + 64 * h
-                x = values[:, pl.ds(pl.multiple_of(r * 128, 128), 128)]
-                halves.append(jnp.where(row == 5, code_ref[pl.ds(r, 8, stride=0), :], x))
-            x = split3(jnp.concatenate(halves, 1))
-            y = lax.dot_general(x, block_permutation(place_ref, j), (((1,), (1,)), ((), ())),
-                                preferred_element_type=F32)
-            ordered[j] = y[0:8] + y[8:16] + y[16:24]
-        return carry
-
-    lax.fori_loop(0, 16, order, 0)
+    def order(j):
+        halves = []
+        for h in range(2):
+            r = j + 64 * h
+            at = r * 128 if isinstance(r, int) else pl.multiple_of(r * 128, 128)
+            x = values[:, pl.ds(at, 128)]
+            halves.append(jnp.where(row == 5, code_ref[pl.ds(r, 8, stride=0), :], x))
+        x = split3(jnp.concatenate(halves, 1))
+        y = lax.dot_general(x, block_permutation(place_ref, j), (((1,), (1,)), ((), ())),
+                            preferred_element_type=F32)
+        return y[0:8] + y[8:16] + y[16:24]
+
+    for step in range(STEPS):
+        ordered[step] = order(step)
     copy.wait()
 
     def append(i, current):
         current = list(current)
-        for step in range(2):
-            j = i * 2 + step
-            y0, y1 = ordered[j, :, 0:128], ordered[j, :, 128:256]
+        ready = [ordered[i * STEPS + step] for step in range(STEPS)]
+        coming = [jnp.minimum((i + 1) * STEPS, 64 - STEPS) + step for step in range(STEPS)]
+        for step in range(STEPS):
+            j = i * STEPS + step
+            y0, y1 = ready[step][:, 0:128], ready[step][:, 128:256]
+            following = order(coming[step])
             for o in range(OWNERS):
                 move, offset = table_s[j, o], table_s[j, 16 + o]
                 tile, end = table_s[j, 32 + o], table_s[j, 48 + o]
@@ -129,9 +136,10 @@
                 stage[pl.ds(at + 8, 8), :] = second
                 stage[pl.ds(at + 16, 8), :] = r1
                 current[o] = jnp.where(end < 128, merged, jnp.where(end < 256, second, r1))
+            ordered[coming[step]] = following
         return tuple(current)
 
-    lax.fori_loop(0, 32, append, tuple(jnp.zeros((8, 128), F32) for _ in range(OWNERS)))
+    lax.fori_loop(0, 64 // STEPS, append, tuple(jnp.zeros((8, 128), F32) for _ in range(OWNERS)))
     for o in range(OWNERS):
         out_ref[o] = stage[pl.ds(o * (TILES + MARGIN) * 8, TILES * 8), :]
 
@@ -437,46 +445,50 @@
     copy.wait()
     lane = iota((8, 128), 1)
 
-    def assemble(i, carry):
-        for step in range(2):
-            j = i * 2 + step
-            acc = [jnp.zeros((8, 128), F32) for _ in range(4)]
-            for o in range(OWNERS):
-                move, offset = table_s[j, o], table_s[j, 16 + o]
-                tile, first = table_s[j, 32 + o], table_s[j, 64 + o]
-                at = pl.multiple_of((o * TILES + tile) * 8, 8)
-                at_last = o * 24 + tile
-                keep = lane >= offset
-                in_low, in_high = lane >= first, lane >= first - 128
-                from_low = lane >= 128 - move
-                from_high = (lane >= -move) & (lane < 128 - move)
-                windows = (
-                    [main[pl.ds(at + 8 * k, 8), :] for k in range(3)],
-                    [last[pl.ds(at_last + k, 8, stride=0), :] for k in range(3)],
-                )
-                for k, (w0, w1, w2) in enumerate(windows):
-                    r0 = pltpu.roll(jnp.where(keep, w0, w2), (-move) & 127, axis=1)
-                    r1 = pltpu.roll(w1, (-move) & 127, axis=1)
-                    acc[2 * k] = jnp.where(in_low, jnp.where(from_low, r1, r0), acc[2 * k])
-                    acc[2 * k + 1] = jnp.where(in_high, jnp.where(from_high, r1, r0), acc[2 * k + 1])
-            for k in range(2):
-                ordered[j, 8 * k:8 * k + 8, 0:128] = acc[2 * k]
-                ordered[j, 8 * k:8 * k + 8, 128:256] = acc[2 * k + 1]
-        return carry
-
-    lax.fori_loop(0, 32, assemble, 0)
+    def assemble(j):
+        acc = [jnp.zeros((8, 128), F32) for _ in range(4)]
+        for o in range(OWNERS):
+            move, offset = table_s[j, o], table_s[j, 16 + o]
+            tile, first = table_s[j, 32 + o], table_s[j, 64 + o]
+            at = pl.multiple_of((o * TILES + tile) * 8, 8)
+            at_last = o * 24 + tile
+            keep = lane >= offset
+            in_low, in_high = lane >= first, lane >= first - 128
+            from_low = lane >= 128 - move
+            from_high = (lane >= -move) & (lane < 128 - move)
+            windows = (
+                [main[pl.ds(at + 8 * k, 8), :] for k in range(3)],
+                [last[pl.ds(at_last + k, 8, stride=0), :] for k in range(3)],
+            )
+            for k, (w0, w1, w2) in enumerate(windows):
+                r0 = pltpu.roll(jnp.where(keep, w0, w2), (-move) & 127, axis=1)
+                r1 = pltpu.roll(w1, (-move) & 127, axis=1)
+                acc[2 * k] = jnp.where(in_low, jnp.where(from_low, r1, r0), acc[2 * k])
+                acc[2 * k + 1] = jnp.where(in_high, jnp.where(from_high, r1, r0), acc[2 * k + 1])
+        return acc
+
+    def keep_block(j, acc):
+        for k in range(2):
+            ordered[j, 8 * k:8 * k + 8, 0:128] = acc[2 * k]
+            ordered[j, 8 * k:8 * k + 8, 128:256] = acc[2 * k + 1]
+
+    for step in range(STEPS):
+        keep_block(step, assemble(step))
 
     def spread(i, carry):
-        for step in range(4):
-            j = i * 4 + step
-            y = jnp.dot(split3(ordered[j]), block_permutation(place_ref, j), preferred_element_type=F32)
+        ready = [ordered[i * STEPS + step] for step in range(STEPS)]
+        for step in range(STEPS):
+            j = i * STEPS + step
+            y = jnp.dot(split3(ready[step]), block_permutation(place_ref, j), preferred_element_type=F32)
             y = y[0:16] + y[16:32] + y[32:48]
             for h in range(2):
                 at = pl.multiple_of((j + 64 * h) * 128, 128)
                 out_ref[:, pl.ds(at, 128)] = y[0:9, h * 128:(h + 1) * 128]
+            coming = jnp.minimum((i + 1) * STEPS, 64 - STEPS) + step
+            keep_block(coming, assemble(coming))
         return carry
 
-    lax.fori_loop(0, 16, spread, 0)
+    lax.fori_loop(0, 64 // STEPS, spread, 0)
 
 
 def collect(main, last, place, table):

time: 97.1 us -> 88.8 us (0.915)
  Pallas kernels: 95.5 us -> 87.3 us
    pallas_call x1, Pallas kernels: 15.6 us -> 10.8 us  [dispatch(): pl.pallas_call(dispatch_kernel, out_shape=[jax.ShapeDtypeStruct((OWNERS,...]
    pallas_call x1, Pallas kernels: 12 us -> 8.64 us  [collect(): pl.pallas_call(collect_kernel, out_shape=jax.ShapeDtypeStruct((9, 16384),...]
where the time goes in v4:
time: 88.8 us; the launch traced here: 88.7 us
  Pallas kernels  87.3 us (98%)
  local copies, waits for them, and re-layouts  1.32 us (1%)
    pallas_call x1, Pallas kernels, place_nodes(): pl.pallas_call(project_kernel, out_shape=[jax.ShapeDtypeStruct((GROUPS *...  67.9 us
    pallas_call x1, Pallas kernels, dispatch(): pl.pallas_call(dispatch_kernel, out_shape=[jax.ShapeDtypeStruct((OWNERS,...  10.8 us
    pallas_call x1, Pallas kernels, collect(): pl.pallas_call(collect_kernel, out_shape=jax.ShapeDtypeStruct((9, 16384),...  8.64 us

profile of v4, /device:TPU:36, one launch (start us, length us, event | category | flops | bytes accessed | tf_op | source)
XLA Modules:
  0.0 88.7 jit_solution(5228108154430110536)
XLA Ops:
  0.0 10.8 %dispatch.1 = (f32[16,160,128]{2,1,0:T(8,128)}, f32[128,128]{1,0:T(8,128)}, s32[64,128]{1,0:T(8,128)}) custom-call(s32[128,128]{1,0:T(8,128)} %bitcast.2, s32[128,128]{1,0:T(8,128)} %bitcast.3, s32[2,16384]{1,0:T(2,128)} %start_hbm.1, f32[3,16384]{1,0:T(4,128)} %target_hbm.1), custom_call_target="tpu_custom_call" | custom-call | tf_op jit(solution)/shard_map/dispatch/pallas_call | solution.py:149
  10.8 0.0 copy-start
  10.8 1.3 %copy-done = f32[16,160,128]{2,1,0:T(8,128)S(1)} copy-done((f32[16,160,128]{2,1,0:T(8,128)S(1)}, f32[16,160,128]{2,1,0:T(8,128)}, u32[]{:S(2)}) %copy-start) | copy-done | bytes 1310744
  12.1 0.0 copy-start.1
  12.1 0.0 copy-start.2
  12.1 67.9 %project.1 = (f32[2584,128]{1,0:T(8,128)S(1)}, f32[384,128]{1,0:T(8,128)S(1)}) custom-call(f32[16,160,128]{2,1,0:T(8,128)S(1)} %copy-done, f32[2500,1024]{1,0:T(8,128)} %net_hbm.1), custom_call_target="tpu_custom_call" | custom-call | tf_op jit(solution)/shard_map/project/pallas_call | solution.py:411
  80.0 0.0 copy-done.1
  80.0 0.0 copy-done.2
  80.1 8.6 %collect.1 = f32[9,16384]{1,0:T(8,128)} custom-call(f32[2584,128]{1,0:T(8,128)S(1)} %get-tuple-element.11.main, f32[384,128]{1,0:T(8,128)S(1)} %get-tuple-element.12.last, f32[128,128]{1,0:T(8,128)S(1)} %copy-done.1, s32[64,128]{1,0:T(8,128)S(1)} %copy-done.2), custom_call_target="tpu_custom_call" | custom-call | tf_op jit(solution)/shard_map/collect/pallas_call | solution.py:497
Async XLA Ops:
  10.8 1.3 %copy-start = (f32[16,160,128]{2,1,0:T(8,128)S(1)}, f32[16,160,128]{2,1,0:T(8,128)}, u32[]{:S(2)}) copy-start(f32[16,160,128]{2,1,0:T(8,128)} %get-tuple-element.10.out_ref) | copy-start | bytes 3932164
  12.1 67.9 %copy-start.1 = (f32[128,128]{1,0:T(8,128)S(1)}, f32[128,128]{1,0:T(8,128)}, u32[]{:S(2)}) copy-start(f32[128,128]{1,0:T(8,128)} %get-tuple-element.13.place_ref) | copy-start | bytes 196612
  12.1 67.9 %copy-start.2 = (s32[64,128]{1,0:T(8,128)S(1)}, s32[64,128]{1,0:T(8,128)}, u32[]{:S(2)}) copy-start(s32[64,128]{1,0:T(8,128)} %get-tuple-element.14.table_hbm) | copy-start | bytes 98308

commit v5 on v4

--- a/solution.py
+++ b/solution.py
@@ -21,6 +21,8 @@
 TILES = 20
 GROUPS = OWNERS * TILES
 MARGIN = 3
+OWN = OWNERS - 1
+FILL = 5
 STEPS = 4
 BATCH = 8
 TURN = 72
@@ -213,7 +215,7 @@
     return a[0] * b[0] + a[1] * b[1] + a[2] * b[2]
 
 
-def project(load, goal, u, v):
+def project(load, goal, u, v, between):
     for _ in range(ITERS):
         p, su, sv = surface(load, u, v)
         miss = [p[c] - goal[c] for c in range(3)]
@@ -222,6 +224,7 @@
         inverse = 1.0 / (a * d - b * b)
         u, v = (jnp.clip(u - (d * gu - b * gv) * inverse, 0.0, 1.0),
                 jnp.clip(v - (a * gv - b * gu) * inverse, 0.0, 1.0))
+        between()
     return surface(load, u, v)
 
 
@@ -241,7 +244,7 @@
 
     for k in range(8):
         net_copy(k).start()
-    first = pltpu.make_async_copy(out_ref.at[me], recv.at[pl.ds(0, SLOT), :], own.at[0])
+    first = pltpu.make_async_copy(out_ref.at[me], recv.at[pl.ds(OWN * SLOT, SLOT), :], own.at[0])
     first.start()
     last[...] = jnp.zeros_like(last)
     pl.semaphore_wait(barrier, OWNERS - 1)
@@ -250,7 +253,7 @@
         peer = lax.rem(me + k, OWNERS)
         return pltpu.make_async_remote_copy(
             src_ref=out_ref.at[peer],
-            dst_ref=recv.at[pl.ds(pl.multiple_of(k * SLOT, 8), SLOT), :],
+            dst_ref=recv.at[pl.ds(pl.multiple_of((k - 1) * SLOT, 8), SLOT), :],
             send_sem=send.at[k], recv_sem=arrive.at[k],
             device_id={"bulk": peer}, device_id_type=MESH,
         )
@@ -259,7 +262,7 @@
         peer = lax.rem(me + OWNERS - k, OWNERS)
         return [
             pltpu.make_async_remote_copy(
-                src_ref=s.at[pl.ds(pl.multiple_of(k * n, 8), n), :],
+                src_ref=s.at[pl.ds(pl.multiple_of((k - 1) * n, 8), n), :],
                 dst_ref=t.at[pl.ds(pl.multiple_of(owner * n, 8), n), :],
                 send_sem=back.at[i, k], recv_sem=home.at[i, k],
                 device_id={"bulk": peer}, device_id_type=MESH,
@@ -268,9 +271,9 @@
         ]
 
     stay = [
-        pltpu.make_async_copy(main.at[pl.ds(0, SLOT), :],
+        pltpu.make_async_copy(main.at[pl.ds(OWN * SLOT, SLOT), :],
                               main_ref.at[pl.ds(pl.multiple_of(me * SLOT, 8), SLOT), :], own.at[1]),
-        pltpu.make_async_copy(last.at[pl.ds(0, 24), :],
+        pltpu.make_async_copy(last.at[pl.ds(OWN * 24, 24), :],
                               last_ref.at[pl.ds(pl.multiple_of(me * 24, 8), 24), :], own.at[2]),
     ]
 
@@ -302,21 +305,22 @@
     def index_copy(b, half):
         return pltpu.make_async_copy(index_v.at[b], (index_a, index_b)[half], index_sem.at[half])
 
-    def gather(index, rows):
-        for h in range(4):
-            for t in range(16):
-                x = None
-                for s in range(8):
-                    for q in range(2):
-                        w = net[pl.ds(index[2 * h + q, t * 8 + s], 8, stride=0), :]
-                        x = w if x is None else jnp.where(masks[s][q], w, x)
-                rows[pl.ds(h * 128 + t * 8, 8), :] = x
-
-    def to_powers(rows, control):
+    def gather(index, rows, begin, end):
+        for unit in range(begin, end):
+            h, t = divmod(unit, 16)
+            x = None
+            for s in range(8):
+                for q in range(2):
+                    w = net[pl.ds(index[2 * h + q, t * 8 + s], 8, stride=0), :]
+                    x = w if x is None else jnp.where(masks[s][q], w, x)
+            rows[pl.ds(h * 128 + t * 8, 8), :] = x
+
+    def to_powers(rows, control, between):
         for h in range(4):
             both = rows[pl.ds(h * 128, 128), :].T
             turned[pl.ds(2 * h * TURN, 64), :] = both[:64]
             turned[pl.ds((2 * h + 1) * TURN, 64), :] = both[64:]
+            between()
         for c in range(4):
             along = [
                 centre(*[turned[pl.ds(c * 16 + i * 4 + j, 8, stride=TURN), :] for i in range(4)])
@@ -325,16 +329,18 @@
             for i in range(4):
                 for j, x in enumerate(centre(*[along[j][i] for j in range(4)])):
                     control[c * 16 + i * 4 + j] = x
+            between()
 
     first.wait()
     outward(1).wait_recv()
+    outward(2).wait_recv()
     prepare(0)
     for half, (index, rows) in enumerate(((index_a, rows_a), (index_b, rows_b))):
         index_copy(half, half).start()
         index_copy(half, half).wait()
-        gather(index, rows)
+        gather(index, rows, 0, 64)
         index_copy(half + 2, half).start()
-    to_powers(rows_a, control_a)
+    to_powers(rows_a, control_a, lambda: None)
 
     def batch(b, half):
         index, rows, other, control, following = (
@@ -344,8 +350,13 @@
         m = lax.div(b, PAIR_BATCHES)
         i = b - m * PAIR_BATCHES
         index_copy(0, half).wait()
-        gather(index, rows)
-        to_powers(other, following)
+        cuts = iter(range(0, 64, FILL))
+
+        def between():
+            at = next(cuts, 64)
+            gather(index, rows, at, min(at + FILL, 64))
+
+        to_powers(other, following, between)
 
         def load(k):
             return control[k]
@@ -353,37 +364,47 @@
         def value(k):
             return recv[pl.ds(b * 64 + k, 8, stride=8), :]
 
-        p, su, sv = project(load, [value(0), value(1), value(2)], value(3), value(4))
+        p, su, sv = project(load, [value(0), value(1), value(2)], value(3), value(4), between)
         for k, x in enumerate((p + su + sv)[:8]):
             main[pl.ds(b * 64 + k, 8, stride=8), :] = x
         last_pair[pl.ds(pl.multiple_of(i * 8, 8), 8), :] = sv[2]
+        between()
 
         @pl.when((i == 1) & (m < OWNERS // 2 - 1))
         def _():
-            outward(2 * m + 2).wait_recv()
             outward(2 * m + 3).wait_recv()
+
+            @pl.when(m < OWNERS // 2 - 2)
+            def _():
+                outward(2 * m + 4).wait_recv()
+
             prepare(m + 1)
 
         index_copy(jnp.minimum(b + 4, BATCHES - 1), half).start()
+
+        def keep_last(h):
+            at = pl.multiple_of((2 * m + h) * 24, 8)
+            last[pl.ds(at, TILES), :] = last_pair[h * TILES:(h + 1) * TILES, :]
+
+        @pl.when(i == 2)
+        def _():
+            keep_last(0)
+            for copy in homeward(2 * m + 1, me):
+                copy.start()
 
         @pl.when(i == PAIR_BATCHES - 1)
         def _():
-            for h in range(2):
-                at = pl.multiple_of((2 * m + h) * 24, 8)
-                last[pl.ds(at, TILES), :] = last_pair[h * TILES:(h + 1) * TILES, :]
-
-            @pl.when(m == 0)
+            keep_last(1)
+
+            @pl.when(m < OWNERS // 2 - 1)
+            def _():
+                for copy in homeward(2 * m + 2, me):
+                    copy.start()
+
+            @pl.when(m == OWNERS // 2 - 1)
             def _():
                 for copy in stay:
                     copy.start()
-
-            @pl.when(m > 0)
-            def _():
-                for copy in homeward(2 * m, me):
-                    copy.start()
-
-            for copy in homeward(2 * m + 1, me):
-                copy.start()
 
     def two(q, carry):
         batch(2 * q, 0)

time: 88.8 us -> 89.1 us (level)
  no operation moved by 1% of the time
where the time goes in v5:
time: 89.1 us; the launch traced here: 88.4 us
  Pallas kernels  87.1 us (98%)
  local copies, waits for them, and re-layouts  1.32 us (1%)
    pallas_call x1, Pallas kernels, place_nodes(): pl.pallas_call(project_kernel, out_shape=[jax.ShapeDtypeStruct((GROUPS *...  67.6 us
    pallas_call x1, Pallas kernels, dispatch(): pl.pallas_call(dispatch_kernel, out_shape=[jax.ShapeDtypeStruct((OWNERS,...  10.8 us
    pallas_call x1, Pallas kernels, collect(): pl.pallas_call(collect_kernel, out_shape=jax.ShapeDtypeStruct((9, 16384),...  8.66 us

profile of v5, /device:TPU:36, one launch (start us, length us, event | category | flops | bytes accessed | tf_op | source)
XLA Modules:
  0.0 88.4 jit_solution(9236718838141732927)
XLA Ops:
  0.0 10.8 %dispatch.1 = (f32[16,160,128]{2,1,0:T(8,128)}, f32[128,128]{1,0:T(8,128)}, s32[64,128]{1,0:T(8,128)}) custom-call(s32[128,128]{1,0:T(8,128)} %bitcast.2, s32[128,128]{1,0:T(8,128)} %bitcast.3, s32[2,16384]{1,0:T(2,128)} %start_hbm.1, f32[3,16384]{1,0:T(4,128)} %target_hbm.1), custom_call_target="tpu_custom_call" | custom-call | tf_op jit(solution)/shard_map/dispatch/pallas_call | solution.py:151
  10.8 0.0 copy-start
  10.8 1.3 %copy-done = f32[16,160,128]{2,1,0:T(8,128)S(1)} copy-done((f32[16,160,128]{2,1,0:T(8,128)S(1)}, f32[16,160,128]{2,1,0:T(8,128)}, u32[]{:S(2)}) %copy-start) | copy-done | bytes 1310744
  12.1 0.0 copy-start.1
  12.1 0.0 copy-start.2
  12.1 67.6 %project.1 = (f32[2584,128]{1,0:T(8,128)S(1)}, f32[384,128]{1,0:T(8,128)S(1)}) custom-call(f32[16,160,128]{2,1,0:T(8,128)S(1)} %copy-done, f32[2500,1024]{1,0:T(8,128)} %net_hbm.1), custom_call_target="tpu_custom_call" | custom-call | tf_op jit(solution)/shard_map/project/pallas_call | solution.py:432
  79.7 0.0 copy-done.1
  79.8 0.0 copy-done.2
  79.8 8.7 %collect.1 = f32[9,16384]{1,0:T(8,128)} custom-call(f32[2584,128]{1,0:T(8,128)S(1)} %get-tuple-element.11.main, f32[384,128]{1,0:T(8,128)S(1)} %get-tuple-element.12.last, f32[128,128]{1,0:T(8,128)S(1)} %copy-done.1, s32[64,128]{1,0:T(8,128)S(1)} %copy-done.2), custom_call_target="tpu_custom_call" | custom-call | tf_op jit(solution)/shard_map/collect/pallas_call | solution.py:518
Async XLA Ops:
  10.8 1.3 %copy-start = (f32[16,160,128]{2,1,0:T(8,128)S(1)}, f32[16,160,128]{2,1,0:T(8,128)}, u32[]{:S(2)}) copy-start(f32[16,160,128]{2,1,0:T(8,128)} %get-tuple-element.10.out_ref) | copy-start | bytes 3932164
  12.1 67.6 %copy-start.1 = (f32[128,128]{1,0:T(8,128)S(1)}, f32[128,128]{1,0:T(8,128)}, u32[]{:S(2)}) copy-start(f32[128,128]{1,0:T(8,128)} %get-tuple-element.13.place_ref) | copy-start | bytes 196612
  12.1 67.6 %copy-start.2 = (s32[64,128]{1,0:T(8,128)S(1)}, s32[64,128]{1,0:T(8,128)}, u32[]{:S(2)}) copy-start(s32[64,128]{1,0:T(8,128)} %get-tuple-element.14.table_hbm) | copy-start | bytes 98308

commit v6 on v5

--- a/solution.py
+++ b/solution.py
@@ -435,7 +435,7 @@
             jax.ShapeDtypeStruct((GROUPS * 8 + 24, 128), F32),
             jax.ShapeDtypeStruct((OWNERS * 24, 128), F32),
         ],
-        in_specs=[vmem, pl.BlockSpec(memory_space=pl.ANY)],
+        in_specs=[pl.BlockSpec(memory_space=pltpu.HBM), pl.BlockSpec(memory_space=pl.ANY)],
         out_specs=[vmem] * 2,
         scratch_shapes=[
             pltpu.VMEM((2 * TABLE, 128), F32),
@@ -528,6 +528,7 @@
 
 def body(node_patch, node_span, start_grid, target, net):
     outgoing, place, table = dispatch(node_patch, node_span, start_grid, target)
+    outgoing = pltpu.with_memory_space_constraint(outgoing, pltpu.HBM)
     main, last = place_nodes(outgoing, net)
     return collect(main, last, place, table)
 

time: 89.1 us -> 87.6 us (0.983)
  local copies, waits for them, and re-layouts: 1.32 us -> 0.01 us
    unnamed x6 -> x4, local copies, waits for them, and re-layouts: 1.32 us -> 0.01 us
where the time goes in v6:
time: 87.6 us; the launch traced here: 87.4 us
  Pallas kernels  87.4 us (100%)
    pallas_call x1, Pallas kernels, place_nodes(): pl.pallas_call(project_kernel, out_shape=[jax.ShapeDtypeStruct((GROUPS *...  67.9 us
    pallas_call x1, Pallas kernels, dispatch(): pl.pallas_call(dispatch_kernel, out_shape=[jax.ShapeDtypeStruct((OWNERS,...  10.8 us
    pallas_call x1, Pallas kernels, collect(): pl.pallas_call(collect_kernel, out_shape=jax.ShapeDtypeStruct((9, 16384),...  8.65 us

profile of v6, /device:TPU:36, one launch (start us, length us, event | category | flops | bytes accessed | tf_op | source)
XLA Modules:
  0.0 87.4 jit_solution(2165328306571909887)
XLA Ops:
  0.0 10.8 %dispatch.1 = (f32[16,160,128]{2,1,0:T(8,128)}, f32[128,128]{1,0:T(8,128)}, s32[64,128]{1,0:T(8,128)}) custom-call(s32[128,128]{1,0:T(8,128)} %bitcast.2, s32[128,128]{1,0:T(8,128)} %bitcast.3, s32[2,16384]{1,0:T(2,128)} %start_hbm.1, f32[3,16384]{1,0:T(4,128)} %target_hbm.1), custom_call_target="tpu_custom_call" | custom-call | tf_op jit(solution)/shard_map/dispatch/pallas_call | solution.py:151
  10.8 0.0 copy-start
  10.8 0.0 copy-start.1
  10.8 67.9 %project.1 = (f32[2584,128]{1,0:T(8,128)S(1)}, f32[384,128]{1,0:T(8,128)S(1)}) custom-call(f32[16,160,128]{2,1,0:T(8,128)} %get-tuple-element.10.out_ref, f32[2500,1024]{1,0:T(8,128)} %net_hbm.1), custom_call_target="tpu_custom_call" | custom-call | tf_op jit(solution)/shard_map/project/pallas_call | solution.py:432
  78.8 0.0 copy-done
  78.8 0.0 copy-done.1
  78.8 8.7 %collect.1 = f32[9,16384]{1,0:T(8,128)} custom-call(f32[2584,128]{1,0:T(8,128)S(1)} %get-tuple-element.11.main, f32[384,128]{1,0:T(8,128)S(1)} %get-tuple-element.12.last, f32[128,128]{1,0:T(8,128)S(1)} %copy-done, s32[64,128]{1,0:T(8,128)S(1)} %copy-done.1), custom_call_target="tpu_custom_call" | custom-call | tf_op jit(solution)/shard_map/collect/pallas_call | solution.py:518
Async XLA Ops:
  10.8 68.0 %copy-start = (f32[128,128]{1,0:T(8,128)S(1)}, f32[128,128]{1,0:T(8,128)}, u32[]{:S(2)}) copy-start(f32[128,128]{1,0:T(8,128)} %get-tuple-element.13.place_ref) | copy-start | bytes 196612
  10.8 68.0 %copy-start.1 = (s32[64,128]{1,0:T(8,128)S(1)}, s32[64,128]{1,0:T(8,128)}, u32[]{:S(2)}) copy-start(s32[64,128]{1,0:T(8,128)} %get-tuple-element.14.table_hbm) | copy-start | bytes 98308
